TPU v7x, 256 devices: a whole 4x4x8 slice. The times are simulated.
256 devices in a mesh: adapter: 32 (over x, y, core), tensor: 8 (over z).
Axes of the slice: x: 4, y: 4, z: 8, core: 2. Of those that a mesh axis runs over, the one named last changes fastest.
Arguments:
- tokens: bfloat16 [2048, 16384], P('tensor', 'adapter'), may hold values from -6 to 6
- query_weight: bfloat16 [16384, 16384], P('adapter', 'tensor'), may hold values from -0.046875 to 0.046875
- adapter_down_factors: bfloat16 [128, 16, 16384], P('adapter'), may hold values from -0.046875 to 0.046875
- adapter_up_factors: bfloat16 [128, 16, 16384], P('adapter'), may hold values from -0.75 to 0.75
- request_combination: int32 [2048], replicated, may hold values from 0 to 511, as said below
- combination_task_ids: int32 [512, 4], replicated, may hold values from 0 to 127, as said below
- combination_coefficient: int32 [512, 4], replicated, may hold values from -4 to 4
Outputs:
- query: bfloat16 [2048, 16384], P('adapter', 'tensor')
Inputs may be any that keep to these rules, and one draw needn't show every extreme that they name: `request_combination`: combination c belongs to owner c // 16. In each aligned block of 256 requests at most 32 requests name combinations of one owner, and one owner, the same for every block, has exactly 32 in every block. `combination_task_ids`: every entry of row c names a task vector of (c // 16) * 4 to (c // 16) * 4 + 3.
All inputs are finite; a program needn't handle non-finite values.
Results may differ from a plain program's by a relative error of at most 0.0042.
Values may be sent and summed in bfloat16 or wider, within the bound.
A program may use at most 128 MiB of HBM per device.

v0:
```python
import jax
import jax.numpy as jnp
from jax import lax
from jax.sharding import PartitionSpec as P


def body(
    tokens,
    query_weight,
    adapter_down_factors,
    adapter_up_factors,
    request_combination,
    combination_task_ids,
    combination_coefficient,
):
    n_owner = lax.axis_size("adapter")
    n_split = lax.axis_size("tensor")
    owner_idx = lax.axis_index("adapter")
    split_idx = lax.axis_index("tensor")
    block_rows = tokens.shape[0]
    total_rows = block_rows * n_split
    req_dev = total_rows // n_owner
    capacity = 4 * req_dev // n_split
    tasks_on_shard = adapter_down_factors.shape[0]
    reduced_activation = adapter_down_factors.shape[1]
    all_combos = combination_task_ids.shape[0]
    combo_dev = all_combos // n_owner
    query_width = adapter_up_factors.shape[2]
    col_width = query_width // n_split
    owners_all = (request_combination // combo_dev).reshape(n_split, block_rows)
    owner_hits = (
        owners_all[:, :, None] == jnp.arange(n_owner, dtype=jnp.int32)[None, None, :]
    ).astype(jnp.int32)
    running_count = jnp.cumsum(owner_hits, axis=1)
    slot_rank = jnp.sum(running_count * owner_hits, axis=2) - 1
    owners_mine = lax.dynamic_index_in_dim(owners_all, split_idx, 0, keepdims=False)
    rank_mine = lax.dynamic_index_in_dim(slot_rank, split_idx, 0, keepdims=False)
    position = owners_mine * capacity + rank_mine
    outgoing = (
        jnp.zeros((n_owner * capacity, tokens.shape[1]), jnp.bfloat16).at[position].set(tokens)
    )
    outgoing = outgoing.reshape(n_owner, capacity, tokens.shape[1])
    received_rows = lax.all_to_all(outgoing, "adapter", split_axis=0, concat_axis=2, tiled=True)
    received_rows = received_rows.reshape(capacity, received_rows.shape[2])
    slot_match = (owners_all == owner_idx)[:, None, :] & (
        slot_rank[:, None, :] == jnp.arange(capacity, dtype=jnp.int32)[None, :, None]
    )
    row_ids = jnp.arange(block_rows, dtype=jnp.int32)[None, None, :]
    slot_row = jnp.sum(jnp.where(slot_match, row_ids, 0), axis=2)
    slot_live = jnp.any(slot_match, axis=2)
    combo_block = request_combination.reshape(n_split, block_rows)
    slot_combo = jnp.sum(jnp.where(slot_match, combo_block[:, None, :], 0), axis=2)
    local_ids = owner_idx * tasks_on_shard + jnp.arange(tasks_on_shard, dtype=jnp.int32)
    task_hits = (combination_task_ids[:, :, None] == local_ids[None, None, :]).astype(jnp.float32)
    weight_table = 0.25 * jnp.sum(
        combination_coefficient.astype(jnp.float32)[:, :, None] * task_hits, axis=1
    )
    combo_here = lax.dynamic_index_in_dim(slot_combo, split_idx, 0, keepdims=False)
    live_here = lax.dynamic_index_in_dim(slot_live, split_idx, 0, keepdims=False)
    chooser = (combo_here[:, None] == jnp.arange(all_combos, dtype=jnp.int32)[None, :]).astype(
        jnp.float32
    )
    slot_weight = jnp.dot(
        chooser, weight_table, precision=lax.Precision.HIGHEST, preferred_element_type=jnp.float32
    )
    slot_weight = slot_weight * live_here.astype(jnp.float32)[:, None]
    query_output = jnp.einsum(
        "ob,hfb->ohf", received_rows, adapter_down_factors, preferred_element_type=jnp.float32
    )
    scaled_low = (
        (query_output * slot_weight[:, :, None])
        .astype(jnp.bfloat16)
        .reshape(capacity, tasks_on_shard * reduced_activation)
    )
    up_factors_flattened = adapter_up_factors.reshape(
        tasks_on_shard * reduced_activation, query_width
    )
    delta_rows = jnp.dot(
        scaled_low, up_factors_flattened, preferred_element_type=jnp.float32
    ).astype(jnp.bfloat16)
    landed = lax.all_to_all(delta_rows, "tensor", split_axis=1, concat_axis=0, tiled=True)
    row_target = jnp.arange(n_split, dtype=jnp.int32)[:, None] * block_rows + slot_row
    row_target = jnp.where(slot_live, row_target, total_rows).reshape(-1)
    delta_dense = (
        jnp.zeros((total_rows, col_width), jnp.float32)
        .at[row_target]
        .add(landed.astype(jnp.float32), mode="drop")
    )
    gathered = lax.all_gather(tokens, "tensor", axis=0, tiled=True)
    summed = lax.psum_scatter(
        jnp.dot(gathered, query_weight, preferred_element_type=jnp.float32) + delta_dense,
        "adapter",
        scatter_dimension=0,
        tiled=True,
    )
    return summed.astype(jnp.bfloat16)


def solution(mesh):
    placed = (
        P("tensor", "adapter"),
        P("adapter", "tensor"),
        P("adapter", None, None),
        P("adapter", None, None),
        P(),
        P(),
        P(),
    )
    return jax.shard_map(
        body, mesh=mesh, in_specs=placed, out_specs=P("adapter", "tensor"), check_vma=False
    )
```

profile of v0, /device:TPU:2, one launch (start us, length us, event | category | flops | bytes accessed | tf_op | source)
XLA Modules:
  0.0 240.2 jit_solution(10887871888954375800)
XLA Ops:
  6.5 0.7 all-gather.2.cloned.1.call-update
  7.3 0.7 add_select_fusion
  8.0 4.6 %reduce-window.6 = s32[8,32,2,128]{3,1,2,0:T(8,128)S(1)} reduce-window(s32[8,32,2,128]{3,1,2,0:T(8,128)S(1)} %fusion.6, s32[]{:T(128)} %constant.32.clone.1), window={size=1x1x1x128 pad=0_0x0_0x0_0x127_0}, to_apply=%region_0.1 | reduce-window | flops 8323072 | bytes 524292 | tf_op jit(solution)/shard_map/reduce-window
  12.7 0.1 slice.8
  12.8 0.2 copy.25
  13.0 0.1 fusion.5
  13.2 3.0 %scatter_custom_fusion = bf16[1024,512]{1,0:T(8,128)(2,1)} fusion(s32[256]{0:T(256)S(1)} %bitcast.57, bf16[256,512]{1,0:T(8,128)(2,1)} %param.7, bf16[]{:T(256)} %constant.61.clone.1), kind=kCustom, calls=%fused_computation.8 | custom fusion | bytes 1049088 | tf_op jit(solution)/shard_map/scatter | solution.py:40
  16.3 7.6 %all-to-all-start = ((bf16[32,32,512]{2,1,0:T(8,128)(2,1)}), bf16[32,32,512]{2,1,0:T(8,128)(2,1)S(1)}, u32[]{:S(2)}, u32[]{:S(2)}) async-start(bf16[32,32,512]{2,1,0:T(8,128)(2,1)} %bitcast.52), calls=%async_computation | async-start | bytes 2097152 | tf_op jit(solution)/shard_map/all_to_all | solution.py:43
  24.0 0.4 select_reduce_fusion
  24.3 0.2 fusion.8
  24.6 0.1 select_reduce_fusion.2
  24.7 0.2 convolution_multiply_fusion.1
  24.9 13.5 %all-to-all-done = bf16[32,32,512]{2,1,0:T(8,128)(2,1)S(1)} async-done(((bf16[32,32,512]{2,1,0:T(8,128)(2,1)}), bf16[32,32,512]{2,1,0:T(8,128)(2,1)S(1)}, u32[]{:S(2)}, u32[]{:S(2)}) %all-to-all-start) | async-done | bytes 1048608 | tf_op jit(solution)/shard_map/all_to_all | solution.py:43
  38.3 1.6 copy.28
  39.9 1.6 reshape.156
  41.5 4.9 %fusion = bf16[32,16384]{1,0:T(8,128)(2,1)} fusion(bf16[4,16,16384]{2,1,0:T(8,128)(2,1)} %param.10, bf16[32,16384,1]{1,0,2:T(8,128)(2,1)S(1)} %reshape.156, bf16[4,16,16384]{2,1,0:T(8,128)(2,1)} %param.9, f32[32,4]{0,1:T(4,128)S(1)} %convolution_multiply_fusion.1), kind=kOutput, calls=%fused_computation.3 | convolution fusion | flops 134746112 | bytes 6291968 | tf_op jit(solution)/shard_map/dot_general | solution.py:78
  46.4 2.4 copy.34
  48.7 8.4 %all-to-all-start.1 = ((bf16[32,8,2048]{2,0,1:T(8,128)(2,1)}), bf16[32,8,2048]{2,0,1:T(8,128)(2,1)S(1)}, u32[]{:S(2)}, u32[]{:S(2)}) async-start(bf16[32,8,2048]{2,0,1:T(8,128)(2,1)} %bitcast.53), calls=%async_computation.1 | async-start | bytes 2097152 | tf_op jit(solution)/shard_map/all_to_all | solution.py:81
  57.4 29.7 %all-to-all-done.1 = bf16[32,8,2048]{2,0,1:T(8,128)(2,1)S(1)} async-done(((bf16[32,8,2048]{2,0,1:T(8,128)(2,1)}), bf16[32,8,2048]{2,0,1:T(8,128)(2,1)S(1)}, u32[]{:S(2)}, u32[]{:S(2)}) %all-to-all-start.1) | async-done | bytes 1048608 | tf_op jit(solution)/shard_map/all_to_all | solution.py:81
  87.1 1.5 convert_element_type.50
  88.6 9.6 %fusion.20 = f32[2048,2048]{1,0:T(8,128)} fusion(bf16[2048,512]{1,0:T(8,128)(2,1)} %all-gather.2.cloned.1.call-done, bf16[512,2048]{1,0:T(8,128)(2,1)S(1)} %copy-done), kind=kOutput, calls=%fused_computation.49 | convolution fusion | flops 4294967296 | bytes 20971520 | tf_op jit(solution)/shard_map/dot_general | solution.py:91
  98.2 16.2 %scatter_fusion = f32[2048,2048]{1,0:T(8,128)} fusion(f32[2048,2048]{1,0:T(8,128)} %fusion.20, s32[256]{0:T(256)S(1)} %bitcast.56, f32[256,2048]{1,0:T(8,128)} %bitcast.50), kind=kCustom, calls=%fused_computation.1 | custom fusion | flops 524288 | bytes 6292480 | tf_op jit(solution)/shard_map/scatter-add | solution.py:87
  114.4 117.2 %reduce-scatter.2.cloned.1.call-done = f32[64,2048]{1,0:T(8,128)} async-done(((f32[2048,2048]{1,0:T(8,128)}), f32[64,2048]{1,0:T(8,128)}) %reduce-scatter.2.cloned.1.call-update) | async-done | bytes 524304 | tf_op jit(solution)/shard_map/reduce_scatter | solution.py:90
  231.6 1.8 convert_element_type.47
  (29 shorter events, 0.4 us)
Async XLA Ops:
  6.5 82.1 %copy-start = (bf16[512,2048]{1,0:T(8,128)(2,1)S(1)}, bf16[512,2048]{1,0:T(8,128)(2,1)}, u32[]{:S(2)}) copy-start(bf16[512,2048]{1,0:T(8,128)(2,1)} %param.8) | copy-start | bytes 6291460
  6.5 82.1 %all-gather.2.cloned.1.call-start = ((), (), s32[]{:S(2)}) async-start(), calls=%async_computation.3 | async-start | bytes 2359296 | tf_op jit(solution)/shard_map/all_gather | solution.py:89
  12.6 11.3 %copy-start.1 = (s32[2048]{0:T(1024)S(1)}, s32[2048]{0:T(1024)}, u32[]{:S(2)}) copy-start(s32[2048]{0:T(1024)} %param.11) | copy-start | bytes 24580
  12.6 11.3 %copy-start.3 = (s32[512,4]{0,1:T(4,128)S(1)}, s32[512,4]{0,1:T(4,128)}, u32[]{:S(2)}) copy-start(s32[512,4]{0,1:T(4,128)} %param.13) | copy-start | bytes 24580
  12.6 11.9 %copy-start.2 = (s32[512,4]{0,1:T(4,128)S(1)}, s32[512,4]{0,1:T(4,128)}, u32[]{:S(2)}) copy-start(s32[512,4]{0,1:T(4,128)} %param.12) | copy-start | bytes 24580
  16.3 22.1 %all-to-all-start = ((bf16[32,32,512]{2,1,0:T(8,128)(2,1)}), bf16[32,32,512]{2,1,0:T(8,128)(2,1)S(1)}, u32[]{:S(2)}, u32[]{:S(2)}) async-start(bf16[32,32,512]{2,1,0:T(8,128)(2,1)} %bitcast.52), calls=%async_computation | async-start | bytes 2097152 | tf_op jit(solution)/shard_map/all_to_all | solution.py:43
  48.7 38.3 %all-to-all-start.1 = ((bf16[32,8,2048]{2,0,1:T(8,128)(2,1)}), bf16[32,8,2048]{2,0,1:T(8,128)(2,1)S(1)}, u32[]{:S(2)}, u32[]{:S(2)}) async-start(bf16[32,8,2048]{2,0,1:T(8,128)(2,1)} %bitcast.53), calls=%async_computation.1 | async-start | bytes 2097152 | tf_op jit(solution)/shard_map/all_to_all | solution.py:81
  57.2 174.4 %reduce-scatter.2.cloned.1.call-start = ((), (), s32[]{:S(2)}) async-start(), calls=%async_computation.4 | async-start | bytes 17301504 | tf_op jit(solution)/shard_map/reduce_scatter | solution.py:90
Sparse Core Ops, SparseCore 0:
  9.1 44.3 all-gather.1
  114.6 117.0 reduce-scatter.1
where the time goes:
time: 241 us; the launch traced here: 240 us
  waiting for transfers between devices  161 us (67%)
  other arithmetic  25.8 us (11%)
  starting transfers between devices  16.1 us (7%)
  matrix products  14.7 us (6%)
  between operations  13.6 us (6%)
  local copies, waits for them, and re-layouts  8.95 us (4%)
    reduce_scatter x1, waiting for transfers between devices, body(): lax.psum_scatter(jnp.dot(gathered, query_weight, preferred_element_type=j...  117 us
    all_to_all x1, waiting for transfers between devices, body(): lax.all_to_all(delta_rows, 'tensor', split_axis=1, concat_axis=0, tiled=T...  29.7 us
    scatter-add x1, other arithmetic, body(): delta_dense = jnp.zeros((total_rows, col_width), jnp.float32).at[row_targ...  16.2 us
    all_to_all x1, waiting for transfers between devices, body(): lax.all_to_all(outgoing, 'adapter', split_axis=0, concat_axis=2, tiled=True)  13.5 us
    dot_general x1, matrix products, body(): jnp.dot(gathered, query_weight, preferred_element_type=jnp.float32)  9.63 us
    all_to_all x1, starting transfers between devices, body(): lax.all_to_all(delta_rows, 'tensor', split_axis=1, concat_axis=0, tiled=T...  8.45 us
    all_to_all x1, starting transfers between devices, body(): lax.all_to_all(outgoing, 'adapter', split_axis=0, concat_axis=2, tiled=True)  7.62 us
    dot_general x1, matrix products, body(): jnp.dot(scaled_low, up_factors_flattened, preferred_element_type=jnp.floa...  4.89 us
  transfers between devices with their start and end apart: 4, of which 3 were waited for; matrix products, arithmetic and copies ran while one was open for 9% of the time, Pallas kernels for 0%

commit v1 on v0

v1 whole, which is shorter than its diff:
```python
import jax
import jax.numpy as jnp
from jax import lax
from jax.experimental import pallas as pl
from jax.experimental.pallas import tpu as pltpu
from jax.sharding import PartitionSpec as P

NX, NY, NZ = 4, 4, 8
NS = 1
RS = 64 // NS
KC = 512
HALF = 1024
QUART = 512
TILE = 256
F32 = jnp.float32
BF16 = jnp.bfloat16


def kernel(
    tok_hbm, w_hbm, a_hbm, b_hbm, rows_ref, ids_ref, coef_ref,
    out_ref,
    tok, wf, a1, a2, bx, by,
    own_n, low_n, lt, lx, ly, low_own, low_all,
    s2, r2, s1, r1, acc, t2, q2, t1, q1,
    send_sem, recv_sem, local_sem,
):
    a_idx = lax.axis_index("adapter")
    z = lax.axis_index("tensor")
    x = a_idx // 8
    y = (a_idx // 2) % 4
    c = a_idx % 2
    other = 1 - c

    def dev(xx, yy, cc, zz):
        return {"adapter": (xx * 4 + yy) * 2 + cc, "tensor": zz}

    def x_peer(k):
        return dev((x + k) % 4, y, c, z)

    def y_peer(k):
        return dev(x, (y + k) % 4, c, z)

    def z_peer(k):
        return dev(x, y, c, (z + k) % 8)

    partner = dev(x, y, other, z)

    counter = [0, 0]

    def remote(src, dst, device):
        i = counter[0]
        counter[0] += 1
        return pltpu.make_async_remote_copy(
            src, dst, send_sem.at[i], recv_sem.at[i],
            device_id=device, device_id_type=pl.DeviceIdType.MESH,
        )

    def local(src, dst):
        i = counter[1]
        counter[1] += 1
        return pltpu.make_async_copy(src, dst, local_sem.at[i])

    sent = []

    def go(copy):
        copy.start()
        sent.append(copy)
        return copy

    my_cols = pl.ds(pl.multiple_of(c * KC, KC), KC)
    tok_local = [
        local(tok_hbm.at[jj, c, s], tok.at[s, 2 * z + jj, :, my_cols])
        for s in range(NS) for jj in range(2)
    ]
    for cp in tok_local:
        cp.start()
    w_local = local(w_hbm, wf.at[my_cols, :])
    w_local.start()
    b_cols = [pl.ds(pl.multiple_of(z * 2048 + h * HALF, HALF), HALF) for h in range(2)]
    b_local = [
        local(b_hbm.at[:, b_cols[0]], bx.at[c, x]),
        local(b_hbm.at[:, b_cols[1]], by.at[c, y]),
    ]
    for cp in b_local:
        cp.start()
    a_wide = lambda xx: pl.ds(pl.multiple_of(xx * 4096, 4096), 4096)
    a_local = local(a_hbm.at[z, :, a_wide(x)], a1.at[x])
    a_local.start()

    barrier = pltpu.get_barrier_semaphore()
    peers = [partner]
    peers += [x_peer(k) for k in range(1, 4)] + [y_peer(k) for k in range(1, 4)]
    peers += [z_peer(k) for k in range(1, 8)]
    for peer in peers:
        pl.semaphore_signal(barrier, inc=1, device_id=peer, device_id_type=pl.DeviceIdType.MESH)
    pl.semaphore_wait(barrier, len(peers))

    tok_pre = [
        go(remote(tok_hbm.at[jj, other, s], tok.at[s, 2 * z + jj, :, my_cols], partner))
        for s in range(NS) for jj in range(2)
    ]
    a_x = [go(remote(a_hbm.at[z, :, a_wide((x + k) % 4)], a1.at[x], x_peer(k))) for k in range(1, 4)]
    w_pre = go(remote(w_hbm, wf.at[my_cols, :], partner))
    b_x = [go(remote(b_hbm.at[:, b_cols[0]], bx.at[c, x], x_peer(k))) for k in range(1, 4)]
    b_y = [go(remote(b_hbm.at[:, b_cols[1]], by.at[c, y], y_peer(k))) for k in range(1, 4)]

    for cp in tok_local:
        cp.wait()
    for cp in tok_pre:
        cp.wait_recv()

    def ring_start(s, k):
        right = (z - k + 8) % 8
        left = (z + k) % 8
        if k < 3:
            src_r = tok.at[s, pl.ds(2 * right, 2)]
            src_l = tok.at[s, pl.ds(2 * left, 2)]
        else:
            src_r = tok.at[s, 2 * right]
            src_l = tok.at[s, 2 * left + 1]
        return go(remote(src_r, src_r, z_peer(1))), go(remote(src_l, src_l, z_peer(7)))

    def ring_wait(pair):
        pair[0].wait_recv()
        pair[1].wait_recv()

    pair = ring_start(0, 0)

    combo = lax.broadcasted_iota(jnp.int32, (512, 4), 0)
    hit = (ids_ref[...] - (combo // 16) * 4) == (z // 2)
    table = 0.25 * jnp.sum(jnp.where(hit, coef_ref[...], 0).astype(F32), axis=1, keepdims=True)
    rows = rows_ref[...]
    weight = jnp.concatenate(
        [
            jnp.sum(
                jnp.where(
                    lax.broadcasted_iota(jnp.int32, (512, 128), 0) == rows[:, 128 * k:128 * (k + 1)],
                    table, 0.0,
                ),
                axis=0, keepdims=True,
            )
            for k in range(8)
        ],
        axis=1,
    )
    owner = rows // 16
    owner_f = owner.astype(F32)
    for k in range(8):
        tile = jnp.broadcast_to(owner_f[:, 128 * k:128 * (k + 1)], (128, 128))
        own_n[128 * k:128 * (k + 1), :] = jnp.transpose(tile)

    a_local.wait()
    for cp in a_x:
        cp.wait_recv()
    a_narrow = lambda yy: pl.ds(pl.multiple_of(yy * 1024, 1024), 1024)
    a_own = local(a1.at[:, :, a_narrow(y)], a2.at[c, y])
    a_own.start()
    a_y = [go(remote(a1.at[:, :, a_narrow((y + k) % 4)], a2.at[c, y], y_peer(k))) for k in range(1, 4)]

    ring_wait(pair)
    pair = ring_start(0, 1)
    a_own.wait()
    for cp in a_y:
        cp.wait_recv()
    a_c = go(remote(a2.at[c], a2.at[c], partner))
    for cp in b_local:
        cp.wait()
    for cp in b_x + b_y:
        cp.wait_recv()
    b_c = [go(remote(bx.at[c], bx.at[c], partner)), go(remote(by.at[c], by.at[c], partner))]
    ring_wait(pair)
    pair = ring_start(0, 2)
    w_local.wait()
    w_pre.wait_recv()
    a_c.wait_recv()
    ring_wait(pair)
    pair = ring_start(0, 3)
    ring_wait(pair)

    af = a2[...].reshape(256, 1024)

    def low_tile(k):
        part = lax.dot_general(
            af, tok[0, 4 * k:4 * (k + 1)].reshape(TILE, 1024), (((1,), (1,)), ((), ())),
            preferred_element_type=F32,
        )
        mine = owner[:, TILE * k:TILE * (k + 1)]
        total = jnp.zeros((8, TILE), F32)
        for g in range(32):
            o = ((g % 4) * 4 + (g // 4) % 4) * 2 + g // 16
            total += jnp.where(mine == o, part[8 * g:8 * (g + 1)], 0.0)
        return total

    for k in range(4):
        lt[:, TILE * k:TILE * (k + 1)] = low_tile(k)
    lo_x = [go(remote(lt, lx.at[k - 1], x_peer(k))) for k in range(1, 4)]

    place = (x, y)
    ring_peer = (x_peer, y_peer)

    def chunk_rows(h, q):
        if h == 0:
            return tok[0, pl.ds(4 * q, 4)].reshape(4 * RS, 1024)
        return jnp.concatenate([tok[0, 4 * j + q] for j in range(4)], axis=0)

    def dots(h, q, first, count, emit):
        lhs = chunk_rows(h, q)
        for n in range(first, first + count):
            cols = slice(h * HALF + n * TILE, h * HALF + (n + 1) * TILE)
            emit(n, jnp.dot(lhs, wf[:, cols], preferred_element_type=F32))

    def cut(n):
        return slice(n * TILE, (n + 1) * TILE)

    lo, hi = pl.ds(0, QUART), pl.ds(QUART, QUART)
    m2 = []
    for h in range(2):
        def put(n, v, h=h):
            s2[h, :, cut(n)] = v.astype(BF16)
        dots(h, (place[h] + 2) % 4, 0, 4, put)
        m2.append((
            go(remote(s2.at[h, :, lo], r2.at[h, 0], ring_peer[h](1))),
            go(remote(s2.at[h, :, hi], r2.at[h, 1], ring_peer[h](3))),
        ))
    m1 = []
    for h in range(2):
        def put_r(n, v, h=h):
            s1[h, 0, :, cut(n)] = v.astype(BF16)
        def put_l(n, v, h=h):
            s1[h, 1, :, cut(n)] = v.astype(BF16)
        dots(h, (place[h] + 1) % 4, 2, 2, put_r)
        m1.append(go(remote(s1.at[h, 0, :, hi], r1.at[h, 0, :, hi], ring_peer[h](1))))
        dots(h, (place[h] + 3) % 4, 0, 2, put_l)
        m1.append(go(remote(s1.at[h, 1, :, lo], r1.at[h, 1, :, lo], ring_peer[h](3))))

    for cp in lo_x:
        cp.wait_recv()
    for cp in lo_x:
        cp.wait_send()
    low_own[...] = (lt[...] + lx[0]) + (lx[1] + lx[2])
    lo_y = [go(remote(low_own, ly.at[k - 1], y_peer(k))) for k in range(1, 4)]

    for h in range(2):
        def keep(n, v, h=h):
            acc[h, :, cut(n)] = v
        dots(h, place[h], 0, 4, keep)
    for h in range(2):
        m2[h][0].wait_recv()
        m2[h][1].wait_recv()
        def add_r(n, v, h=h):
            s1[h, 0, :, cut(n)] = (v + r2[h, 0, :, cut(n)].astype(F32)).astype(BF16)
        def add_l(n, v, h=h):
            s1[h, 1, :, cut(n)] = (v + r2[h, 1, :, cut(n - 2)].astype(F32)).astype(BF16)
        dots(h, (place[h] + 1) % 4, 0, 2, add_r)
        m1.append(go(remote(s1.at[h, 0, :, lo], r1.at[h, 0, :, lo], ring_peer[h](1))))
        dots(h, (place[h] + 3) % 4, 2, 2, add_l)
        m1.append(go(remote(s1.at[h, 1, :, hi], r1.at[h, 1, :, hi], ring_peer[h](3))))

    for cp in lo_y:
        cp.wait_recv()
    total = (low_own[...] + ly[0]) + (ly[1] + ly[2])
    low_all[z] = (total * weight).astype(BF16)
    lo_z = [go(remote(low_all.at[z], low_all.at[z], z_peer(k))) for k in range(1, 8)]
    for cp in lo_z:
        cp.wait_recv()
    low_t = low_all[...].astype(F32).reshape(64, 1024)
    for k in range(8):
        tile = low_t[:, 128 * k:128 * (k + 1)]
        low_n[128 * k:128 * (k + 1), :] = jnp.transpose(jnp.concatenate([tile, tile], axis=0))

    for cp in b_c:
        cp.wait_recv()
    for cp in m1:
        cp.wait_recv()
    lane = lax.broadcasted_iota(jnp.int32, (4 * RS, 128), 1)

    def masked(h):
        if h == 0:
            at = pl.ds(pl.multiple_of(x * 4 * RS, 4 * RS), 4 * RS)
            ow, lw = own_n[at, :], low_n[at, :]
        else:
            ats = [pl.ds(pl.multiple_of((4 * j + y) * RS, RS), RS) for j in range(4)]
            ow = jnp.concatenate([own_n[at, :] for at in ats], axis=0)
            lw = jnp.concatenate([low_n[at, :] for at in ats], axis=0)
        pieces = []
        for cc in range(2):
            for m in range(2):
                if h == 0:
                    o0, step = ((2 * m) * 4 + y) * 2 + cc, 8
                else:
                    o0, step = (x * 4 + 2 * m) * 2 + cc, 2
                want = jnp.where(lane < 64, o0, o0 + step).astype(F32)
                pieces.append(jnp.where(ow == want, lw, 0.0).astype(BF16))
        return jnp.concatenate(pieces, axis=1)

    for h in range(2):
        lhs = masked(h)
        up = (bx, by)[h]
        for n in range(4):
            delta = jnp.dot(
                lhs, up[:, :, :, cut(n)].reshape(512, TILE), preferred_element_type=F32
            )
            acc[h, :, cut(n)] = (acc[h, :, cut(n)] + delta) + (
                r1[h, 0, :, cut(n)].astype(F32) + r1[h, 1, :, cut(n)].astype(F32)
            )

    place2 = (y, x)
    peer2 = (y_peer, x_peer)

    def block(h, q):
        return pl.ds(pl.multiple_of(q * RS, RS), RS)

    n2, n1 = [], []
    for h in range(2):
        t2[h] = acc[h, block(h, (place2[h] + 2) % 4), :].astype(BF16)
        n2.append((
            go(remote(t2.at[h, :, lo], q2.at[h, 0], peer2[h](1))),
            go(remote(t2.at[h, :, hi], q2.at[h, 1], peer2[h](3))),
        ))
    for h in range(2):
        t1[h, 0, :, QUART:] = acc[h, block(h, (place2[h] + 1) % 4), QUART:].astype(BF16)
        n1.append(go(remote(t1.at[h, 0, :, hi], q1.at[h, 0, :, hi], peer2[h](1))))
        t1[h, 1, :, :QUART] = acc[h, block(h, (place2[h] + 3) % 4), :QUART].astype(BF16)
        n1.append(go(remote(t1.at[h, 1, :, lo], q1.at[h, 1, :, lo], peer2[h](3))))
    for h in range(2):
        n2[h][0].wait_recv()
        n2[h][1].wait_recv()
        t1[h, 0, :, :QUART] = (
            acc[h, block(h, (place2[h] + 1) % 4), :QUART] + q2[h, 0].astype(F32)
        ).astype(BF16)
        n1.append(go(remote(t1.at[h, 0, :, lo], q1.at[h, 0, :, lo], peer2[h](1))))
        t1[h, 1, :, QUART:] = (
            acc[h, block(h, (place2[h] + 3) % 4), QUART:] + q2[h, 1].astype(F32)
        ).astype(BF16)
        n1.append(go(remote(t1.at[h, 1, :, hi], q1.at[h, 1, :, hi], peer2[h](3))))
    for cp in n1:
        cp.wait_recv()
    for h in range(2):
        out_ref[:, h * HALF:(h + 1) * HALF] = (
            acc[h, block(h, place2[h]), :] + (q1[h, 0].astype(F32) + q1[h, 1].astype(F32))
        ).astype(BF16)
    for cp in sent:
        if all(cp is not done for done in lo_x):
            cp.wait_send()


def body(tokens, query_weight, down, up, request_combination, task_ids, coefficient):
    c = lax.axis_index("adapter") % 2
    rows = lax.dynamic_index_in_dim(
        request_combination.reshape(16, 2, NS, RS), c, 1, keepdims=False
    )
    rows = rows.transpose(1, 0, 2).reshape(1, 1024)
    hbm = pl.BlockSpec(memory_space=pl.ANY)
    vmem = pl.BlockSpec(memory_space=pltpu.VMEM)
    n_sem = 96
    return pl.pallas_call(
        kernel,
        out_shape=jax.ShapeDtypeStruct((64, 2048), BF16),
        in_specs=[hbm, hbm, hbm, hbm, vmem, vmem, vmem],
        out_specs=vmem,
        scratch_shapes=[
            pltpu.VMEM((NS, 16, RS, 1024), BF16),
            pltpu.VMEM((1024, 2048), BF16),
            pltpu.VMEM((4, 8, 4096), BF16),
            pltpu.VMEM((2, 4, 4, 8, 1024), BF16),
            pltpu.VMEM((2, 4, 64, HALF), BF16),
            pltpu.VMEM((2, 4, 64, HALF), BF16),
            pltpu.VMEM((1024, 128), F32),
            pltpu.VMEM((1024, 128), F32),
            pltpu.VMEM((8, 1024), F32),
            pltpu.VMEM((3, 8, 1024), F32),
            pltpu.VMEM((3, 8, 1024), F32),
            pltpu.VMEM((8, 1024), F32),
            pltpu.VMEM((8, 8, 1024), BF16),
            pltpu.VMEM((2, 4 * RS, HALF), BF16),
            pltpu.VMEM((2, 2, 4 * RS, QUART), BF16),
            pltpu.VMEM((2, 2, 4 * RS, HALF), BF16),
            pltpu.VMEM((2, 2, 4 * RS, HALF), BF16),
            pltpu.VMEM((2, 4 * RS, HALF), F32),
            pltpu.VMEM((2, RS, HALF), BF16),
            pltpu.VMEM((2, 2, RS, QUART), BF16),
            pltpu.VMEM((2, 2, RS, HALF), BF16),
            pltpu.VMEM((2, 2, RS, HALF), BF16),
            pltpu.SemaphoreType.DMA((n_sem,)),
            pltpu.SemaphoreType.DMA((n_sem,)),
            pltpu.SemaphoreType.DMA((16,)),
        ],
        compiler_params=pltpu.CompilerParams(
            collective_id=0, has_side_effects=True, vmem_limit_bytes=48 * 1024 * 1024
        ),
    )(
        tokens.reshape(2, 2, NS, RS, KC),
        query_weight,
        down.reshape(8, 8, 16384),
        up.reshape(64, 16384),
        rows,
        task_ids,
        coefficient,
    )


def solution(mesh):
    placed = (
        P("tensor", "adapter"),
        P("adapter", "tensor"),
        P("adapter", None, None),
        P("adapter", None, None),
        P(),
        P(),
        P(),
    )
    return jax.shard_map(
        body, mesh=mesh, in_specs=placed, out_specs=P("adapter", "tensor"), check_vma=False
    )
```

time: 241 us -> 80.1 us (0.33)
  waiting for transfers between devices: 161 us -> 0 us
  Pallas kernels: 0 us -> 72.4 us
  other arithmetic: 25.8 us -> 0 us
  starting transfers between devices: 16.1 us -> 0 us
  matrix products: 14.7 us -> 0 us
  between operations: 13.6 us -> 0.04 us
    reduce_scatter x1 -> x0, waiting for transfers between devices: 117 us -> none  [body(): lax.psum_scatter(jnp.dot(gathered, query_weight, preferred_element_type=j...]
    pallas_call x0 -> x1, Pallas kernels: none -> 72.4 us  [body(): pl.pallas_call(kernel, out_shape=jax.ShapeDtypeStruct((64, 2048), BF16),...]
    all_to_all x2 -> x0, waiting for transfers between devices: 43.1 us -> none  [the longest x1 29.7 us: body(): lax.all_to_all(delta_rows, 'tensor', split_axis=1, concat_axis=0, tiled=T...]
    scatter-add x1 -> x0, other arithmetic: 16.2 us -> none  [body(): delta_dense = jnp.zeros((total_rows, col_width), jnp.float32).at[row_targ...]
    all_to_all x2 -> x0, starting transfers between devices: 16.1 us -> none  [the longest x1 8.45 us: body(): lax.all_to_all(delta_rows, 'tensor', split_axis=1, concat_axis=0, tiled=T...]
    dot_general x3 -> x0, matrix products: 14.7 us -> none  [the longest x1 9.63 us: body(): jnp.dot(gathered, query_weight, preferred_element_type=jnp.float32)]
    unnamed x8 -> x9, local copies, waits for them, and re-layouts: 0.02 us -> 6.51 us
    another operation x2 -> x0, other arithmetic: 4.69 us -> none
  transfers between devices with their start and end apart: 4 -> 0, of which waited for: 3 -> 0; matrix products, arithmetic and copies ran while one was open for 9% -> 0% of each run, Pallas kernels for 0% -> 0%
where the time goes in v1:
time: 80.1 us; the launch traced here: 79.8 us
  Pallas kernels  72.4 us (90%)
  local copies, waits for them, and re-layouts  7.39 us (9%)
    pallas_call x1, Pallas kernels, body(): pl.pallas_call(kernel, out_shape=jax.ShapeDtypeStruct((64, 2048), BF16),...  72.4 us
    unnamed x9, local copies, waits for them, and re-layouts  6.51 us

profile of v1, /device:TPU:2, one launch (start us, length us, event | category | flops | bytes accessed | tf_op | source)
XLA Modules:
  0.0 79.8 jit_solution(13753308981080292739)
XLA Ops:
  0.0 0.8 reshape.16
  0.8 0.1 reshape_transpose.3.rows_ref
  0.9 0.8 %copy.10.ids_ref = s32[512,4]{1,0:T(8,128)S(1)} copy(s32[512,4]{0,1:T(4,128)} %param.12) | data formatting | bytes 16384 | tf_op args[5]
  1.7 0.8 %copy.11.coef_ref = s32[512,4]{1,0:T(8,128)S(1)} copy(s32[512,4]{0,1:T(4,128)} %param.13) | data formatting | bytes 16384 | tf_op args[6]
  2.6 0.0 copy-start
  2.6 1.6 %copy-done = bf16[512,2048]{1,0:T(8,128)(2,1)S(1)} copy-done((bf16[512,2048]{1,0:T(8,128)(2,1)S(1)}, bf16[512,2048]{1,0:T(8,128)(2,1)}, u32[]{:S(2)}) %copy-start) | copy-done | bytes 2097176
  4.2 0.0 copy-start.1
  4.2 1.6 %copy-done.1 = bf16[4,16,16384]{2,1,0:T(8,128)(2,1)S(1)} copy-done((bf16[4,16,16384]{2,1,0:T(8,128)(2,1)S(1)}, bf16[4,16,16384]{2,1,0:T(8,128)(2,1)}, u32[]{:S(2)}) %copy-start.1) | copy-done | bytes 2097176
  5.8 0.0 copy-start.2
  5.8 0.9 %copy-done.2 = bf16[256,512]{1,0:T(8,128)(2,1)S(1)} copy-done((bf16[256,512]{1,0:T(8,128)(2,1)S(1)}, bf16[256,512]{1,0:T(8,128)(2,1)}, u32[]{:S(2)}) %copy-start.2) | copy-done | bytes 262168
  6.7 72.4 %shard_map.73 = bf16[64,2048]{1,0:T(8,128)(2,1)S(1)} custom-call(bf16[2,2,1,64,512]{4,3,2,1,0:T(8,128)(2,1)S(1)} %bitcast.4, bf16[512,2048]{1,0:T(8,128)(2,1)S(1)} %copy-done, bf16[8,8,16384]{2,1,0:T(8,128)(2,1)S(1)} %bitcast.3, bf16[64,16384]{1,0:T(8,128)(2,1)} %bitcast.5, s32[1,1024]{1,0:T(1,128)S(1)} %reshape_transpose.3.rows_ref, ...), custom_call_target="tpu_custom_call" | custom-call | tf_op jit(solution)/shard_map/pallas_call | solution.py:356
  79.1 0.7 copy.13
  (1 shorter events, 0.0 us)
Async XLA Ops:
  2.6 1.6 %copy-start = (bf16[512,2048]{1,0:T(8,128)(2,1)S(1)}, bf16[512,2048]{1,0:T(8,128)(2,1)}, u32[]{:S(2)}) copy-start(bf16[512,2048]{1,0:T(8,128)(2,1)} %w_hbm.1) | copy-start | bytes 6291460
  4.2 1.6 %copy-start.1 = (bf16[4,16,16384]{2,1,0:T(8,128)(2,1)S(1)}, bf16[4,16,16384]{2,1,0:T(8,128)(2,1)}, u32[]{:S(2)}) copy-start(bf16[4,16,16384]{2,1,0:T(8,128)(2,1)} %param.9) | copy-start | bytes 6291460
  5.8 0.9 %copy-start.2 = (bf16[256,512]{1,0:T(8,128)(2,1)S(1)}, bf16[256,512]{1,0:T(8,128)(2,1)}, u32[]{:S(2)}) copy-start(bf16[256,512]{1,0:T(8,128)(2,1)} %param.7) | copy-start | bytes 786436

commit v2 on v0

v2 whole, which is shorter than its diff:
```python
import jax
import jax.numpy as jnp
from jax import lax
from jax.experimental import pallas as pl
from jax.experimental.pallas import tpu as pltpu
from jax.sharding import PartitionSpec as P

NS = 2
RS = 64 // NS
SR = 16 * RS
CR = 4 * RS
KC = 512
HALF = 1024
QUART = 512
TILE = 256
F32 = jnp.float32
BF16 = jnp.bfloat16


def kernel(
    tok_hbm, w_hbm, a_hbm, b_hbm, rows_ref, ids_ref, coef_ref,
    out_ref,
    tok, wf, a1, a2, bx, by,
    own_n, low_n, lt, lx, ly, low_own, low_all,
    s2, r2, s1, r1, acc, t2, q2, t1, q1,
    send_sem, recv_sem, local_sem,
):
    a_idx = lax.axis_index("adapter")
    z = lax.axis_index("tensor")
    x = a_idx // 8
    y = (a_idx // 2) % 4
    c = a_idx % 2
    other = 1 - c

    def dev(xx, yy, cc, zz):
        return {"adapter": (xx * 4 + yy) * 2 + cc, "tensor": zz}

    def x_peer(k):
        return dev((x + k) % 4, y, c, z)

    def y_peer(k):
        return dev(x, (y + k) % 4, c, z)

    def z_peer(k):
        return dev(x, y, c, (z + k) % 8)

    partner = dev(x, y, other, z)
    counter = [0, 0]
    sent = []

    def go(src, dst, device):
        i = counter[0]
        counter[0] += 1
        copy = pltpu.make_async_remote_copy(
            src, dst, send_sem.at[i], recv_sem.at[i],
            device_id=device, device_id_type=pl.DeviceIdType.MESH,
        )
        copy.start()
        sent.append(copy)
        return copy

    def local(src, dst):
        i = counter[1]
        counter[1] += 1
        copy = pltpu.make_async_copy(src, dst, local_sem.at[i])
        copy.start()
        return copy

    def arrived(copies):
        for cp in copies:
            cp.wait_recv()

    my_cols = pl.ds(pl.multiple_of(c * KC, KC), KC)
    tok_local = [
        local(tok_hbm.at[jj, c, s], tok.at[s, 2 * z + jj, :, my_cols])
        for s in range(NS) for jj in range(2)
    ]
    a_wide = lambda xx: pl.ds(pl.multiple_of(xx * 4096, 4096), 4096)
    a_narrow = lambda yy: pl.ds(pl.multiple_of(yy * 1024, 1024), 1024)
    a_local = local(a_hbm.at[z, :, a_wide(x)], a1.at[x])
    b_cols = [pl.ds(pl.multiple_of(z * 2048 + h * HALF, HALF), HALF) for h in range(2)]
    b_local = [
        local(b_hbm.at[:, b_cols[0]], bx.at[c, x]),
        local(b_hbm.at[:, b_cols[1]], by.at[c, y]),
    ]
    w_local = local(w_hbm, wf.at[my_cols, :])

    barrier = pltpu.get_barrier_semaphore()
    peers = [partner]
    peers += [x_peer(k) for k in range(1, 4)] + [y_peer(k) for k in range(1, 4)]
    peers += [z_peer(k) for k in range(1, 8)]
    for peer in peers:
        pl.semaphore_signal(barrier, inc=1, device_id=peer, device_id_type=pl.DeviceIdType.MESH)

    lane8 = lax.broadcasted_iota(jnp.int32, (8, 128), 1)
    per = 128 // RS
    groups = []
    for s in range(NS):
        for g in range(16 // per):
            piece = jnp.zeros((8, 128), jnp.int32)
            for j in range(per):
                d = per * g + j
                raw = jnp.broadcast_to(rows_ref[:, 128 * d:128 * (d + 1)], (8, 128))
                shift = (RS * j - RS * s + 256 - 64 * c) % 128
                piece = jnp.where(lane8 // RS == j, pltpu.roll(raw, shift, 1), piece)
            groups.append(piece[0:1])

    combo = lax.broadcasted_iota(jnp.int32, (4, 512), 1)
    hit = (ids_ref[...] - (combo // 16) * 4) == (z // 2)
    table = 0.25 * jnp.sum(jnp.where(hit, coef_ref[...], 0).astype(F32), axis=0, keepdims=True)
    column = jnp.concatenate(
        [
            jnp.transpose(jnp.broadcast_to(table[:, 128 * k:128 * (k + 1)], (128, 128)))
            for k in range(4)
        ],
        axis=0,
    )
    number = lax.broadcasted_iota(jnp.int32, (512, 128), 0)
    weight = jnp.concatenate(
        [
            jnp.sum(jnp.where(number == g, column, 0.0), axis=0, keepdims=True)
            for g in groups
        ],
        axis=1,
    )
    rows = jnp.concatenate(groups, axis=1)
    owner = rows // 16
    owner_f = owner.astype(F32)
    for k in range(8):
        tile = jnp.broadcast_to(owner_f[:, 128 * k:128 * (k + 1)], (128, 128))
        own_n[128 * k:128 * (k + 1), :] = jnp.transpose(tile)

    pl.semaphore_wait(barrier, len(peers))

    tok_pre = [
        go(tok_hbm.at[jj, other, s], tok.at[s, 2 * z + jj, :, my_cols], partner)
        for s in range(NS) for jj in range(2)
    ]
    a_x = [go(a_hbm.at[z, :, a_wide((x + k) % 4)], a1.at[x], x_peer(k)) for k in range(1, 4)]
    w_pre = go(w_hbm, wf.at[my_cols, :], partner)
    b_x = [go(b_hbm.at[:, b_cols[0]], bx.at[c, x], x_peer(k)) for k in range(1, 4)]
    b_y = [go(b_hbm.at[:, b_cols[1]], by.at[c, y], y_peer(k)) for k in range(1, 4)]

    moving = {}

    def ring(s, k):
        for u in range(2):
            ways = ("r", "l") if k < 3 else (("r",), ("l",))[u]
            for way in ways:
                if k > 0:
                    moving.pop((s, k - 1, u, way)).wait_recv()
                b = (z - k + 8) % 8 if way == "r" else (z + k) % 8
                src = tok.at[s, 2 * b + u]
                moving[s, k, u, way] = go(src, src, z_peer(1 if way == "r" else 7))

    def ring_end(s):
        for key in [key for key in moving if key[0] == s]:
            moving.pop(key).wait_recv()

    def low_part(s):
        af = a2[...].reshape(256, 1024)
        for k in range(SR // TILE):
            nd = TILE // RS
            part = lax.dot_general(
                af, tok[s, nd * k:nd * (k + 1)].reshape(TILE, 1024),
                (((1,), (1,)), ((), ())), preferred_element_type=F32,
            )
            mine = owner[:, s * SR + TILE * k:s * SR + TILE * (k + 1)]
            total = jnp.zeros((8, TILE), F32)
            for g in range(32):
                o = ((g % 4) * 4 + (g // 4) % 4) * 2 + g // 16
                total += jnp.where(mine == o, part[8 * g:8 * (g + 1)], 0.0)
            lt[s, :, TILE * k:TILE * (k + 1)] = total
        return [go(lt.at[s], lx.at[s, k - 1], x_peer(k)) for k in range(1, 4)]

    def low_x(s, copies):
        arrived(copies)
        low_own[s] = (lt[s] + lx[s, 0]) + (lx[s, 1] + lx[s, 2])
        return [go(low_own.at[s], ly.at[s, k - 1], y_peer(k)) for k in range(1, 4)]

    def low_y(s, copies):
        arrived(copies)
        total = (low_own[s] + ly[s, 0]) + (ly[s, 1] + ly[s, 2])
        low_all[s, z] = (total * weight[:, s * SR:(s + 1) * SR]).astype(BF16)
        return [go(low_all.at[s, z], low_all.at[s, z], z_peer(k)) for k in (4, 3, 5, 2, 6, 1, 7)]

    def low_z(s, copies):
        arrived(copies)
        low_t = low_all[s].astype(F32).reshape(64, SR)
        for k in range(SR // 128):
            tile = low_t[:, 128 * k:128 * (k + 1)]
            low_n[s * SR + 128 * k:s * SR + 128 * (k + 1), :] = jnp.transpose(
                jnp.concatenate([tile, tile], axis=0)
            )

    place = (x, y)
    ring_peer = (x_peer, y_peer)

    def cut(n):
        return slice(n * TILE, (n + 1) * TILE)

    lo, hi = pl.ds(0, QUART), pl.ds(QUART, QUART)

    def dots(s, h, q, first, count, emit):
        if h == 0:
            lhs = tok[s, pl.ds(4 * q, 4)].reshape(CR, 1024)
        else:
            lhs = jnp.concatenate([tok[s, 4 * j + q] for j in range(4)], axis=0)
        for n in range(first, first + count):
            cols = slice(h * HALF + n * TILE, h * HALF + (n + 1) * TILE)
            emit(n, jnp.dot(lhs, wf[:, cols], preferred_element_type=F32))

    def far(s):
        out = []
        for h in range(2):
            def put(n, v, h=h):
                s2[s, h, :, cut(n)] = v.astype(BF16)
            dots(s, h, (place[h] + 2) % 4, 0, 4, put)
            out.append(go(s2.at[s, h, :, lo], r2.at[s, h, 0], ring_peer[h](1)))
            out.append(go(s2.at[s, h, :, hi], r2.at[s, h, 1], ring_peer[h](3)))
        return out

    def near(s):
        out = []
        for h in range(2):
            def put_r(n, v, h=h):
                s1[s, h, 0, :, cut(n)] = v.astype(BF16)
            def put_l(n, v, h=h):
                s1[s, h, 1, :, cut(n)] = v.astype(BF16)
            dots(s, h, (place[h] + 1) % 4, 2, 2, put_r)
            out.append(go(s1.at[s, h, 0, :, hi], r1.at[s, h, 0, :, hi], ring_peer[h](1)))
            dots(s, h, (place[h] + 3) % 4, 0, 2, put_l)
            out.append(go(s1.at[s, h, 1, :, lo], r1.at[s, h, 1, :, lo], ring_peer[h](3)))
        return out

    def keep(s):
        for h in range(2):
            def put(n, v, h=h):
                acc[s, h, :, cut(n)] = v
            dots(s, h, place[h], 0, 4, put)

    def relay(s, copies):
        out = []
        for h in range(2):
            arrived(copies[2 * h:2 * h + 2])
            def add_r(n, v, h=h):
                s1[s, h, 0, :, cut(n)] = (v + r2[s, h, 0, :, cut(n)].astype(F32)).astype(BF16)
            def add_l(n, v, h=h):
                s1[s, h, 1, :, cut(n)] = (v + r2[s, h, 1, :, cut(n - 2)].astype(F32)).astype(BF16)
            dots(s, h, (place[h] + 1) % 4, 0, 2, add_r)
            out.append(go(s1.at[s, h, 0, :, lo], r1.at[s, h, 0, :, lo], ring_peer[h](1)))
            dots(s, h, (place[h] + 3) % 4, 2, 2, add_l)
            out.append(go(s1.at[s, h, 1, :, hi], r1.at[s, h, 1, :, hi], ring_peer[h](3)))
        return out

    lane = lax.broadcasted_iota(jnp.int32, (CR, 128), 1)

    def masked(s, h):
        if h == 0:
            at = pl.ds(pl.multiple_of(s * SR + x * CR, CR), CR)
            ow, lw = own_n[at, :], low_n[at, :]
        else:
            ats = [pl.ds(pl.multiple_of(s * SR + (4 * j + y) * RS, RS), RS) for j in range(4)]
            ow = jnp.concatenate([own_n[at, :] for at in ats], axis=0)
            lw = jnp.concatenate([low_n[at, :] for at in ats], axis=0)
        pieces = []
        for cc in range(2):
            for m in range(2):
                if h == 0:
                    o0, step = ((2 * m) * 4 + y) * 2 + cc, 8
                else:
                    o0, step = (x * 4 + 2 * m) * 2 + cc, 2
                want = jnp.where(lane < 64, o0, o0 + step).astype(F32)
                pieces.append(jnp.where(ow == want, lw, 0.0).astype(BF16))
        return jnp.concatenate(pieces, axis=1)

    place2 = (y, x)
    peer2 = (y_peer, x_peer)

    def block(h, q):
        return pl.ds(pl.multiple_of(q * RS, RS), RS)

    def collect(s, copies):
        arrived(copies)
        out = []
        for h in range(2):
            lhs = masked(s, h)
            up = (bx, by)[h]
            for n in range(4):
                delta = jnp.dot(
                    lhs, up[:, :, :, cut(n)].reshape(512, TILE), preferred_element_type=F32
                )
                acc[s, h, :, cut(n)] = (acc[s, h, :, cut(n)] + delta) + (
                    r1[s, h, 0, :, cut(n)].astype(F32) + r1[s, h, 1, :, cut(n)].astype(F32)
                )
            t2[s, h] = acc[s, h, block(h, (place2[h] + 2) % 4), :].astype(BF16)
            out.append(go(t2.at[s, h, :, lo], q2.at[s, h, 0], peer2[h](1)))
            out.append(go(t2.at[s, h, :, hi], q2.at[s, h, 1], peer2[h](3)))
        return out

    def near2(s):
        out = []
        for h in range(2):
            t1[s, h, 0, :, QUART:] = acc[s, h, block(h, (place2[h] + 1) % 4), QUART:].astype(BF16)
            out.append(go(t1.at[s, h, 0, :, hi], q1.at[s, h, 0, :, hi], peer2[h](1)))
            t1[s, h, 1, :, :QUART] = acc[s, h, block(h, (place2[h] + 3) % 4), :QUART].astype(BF16)
            out.append(go(t1.at[s, h, 1, :, lo], q1.at[s, h, 1, :, lo], peer2[h](3)))
        return out

    def relay2(s, copies):
        out = []
        for h in range(2):
            arrived(copies[2 * h:2 * h + 2])
            t1[s, h, 0, :, :QUART] = (
                acc[s, h, block(h, (place2[h] + 1) % 4), :QUART] + q2[s, h, 0].astype(F32)
            ).astype(BF16)
            out.append(go(t1.at[s, h, 0, :, lo], q1.at[s, h, 0, :, lo], peer2[h](1)))
            t1[s, h, 1, :, QUART:] = (
                acc[s, h, block(h, (place2[h] + 3) % 4), QUART:] + q2[s, h, 1].astype(F32)
            ).astype(BF16)
            out.append(go(t1.at[s, h, 1, :, hi], q1.at[s, h, 1, :, hi], peer2[h](3)))
        return out

    def finish(s, copies):
        arrived(copies)
        for h in range(2):
            out_ref[s * RS:(s + 1) * RS, h * HALF:(h + 1) * HALF] = (
                acc[s, h, block(h, place2[h]), :]
                + (q1[s, h, 0].astype(F32) + q1[s, h, 1].astype(F32))
            ).astype(BF16)

    for cp in tok_local:
        cp.wait()
    arrived(tok_pre[:2])
    ring(0, 0)
    arrived(tok_pre[2:])
    a_local.wait()
    arrived(a_x)
    a_own = local(a1.at[:, :, a_narrow(y)], a2.at[c, y])
    a_y = [go(a1.at[:, :, a_narrow((y + k) % 4)], a2.at[c, y], y_peer(k)) for k in range(1, 4)]
    ring(0, 1)
    for cp in b_local:
        cp.wait()
    ring(0, 2)
    a_own.wait()
    arrived(a_y)
    a_c = go(a2.at[c], a2.at[c], partner)
    arrived(b_x + b_y)
    b_c = [go(bx.at[c], bx.at[c], partner), go(by.at[c], by.at[c], partner)]
    ring(0, 3)
    ring(1, 0)
    w_local.wait()
    arrived([w_pre, a_c])
    ring_end(0)

    lo0 = low_part(0)
    far0 = far(0)
    ring(1, 1)
    m0 = near(0)
    lo0 = low_x(0, lo0)
    ring(1, 2)
    keep(0)
    m0 += relay(0, far0)
    lo0 = low_y(0, lo0)
    ring(1, 3)
    arrived(b_c)
    low_z(0, lo0)
    ring_end(1)

    lo1 = low_part(1)
    far1 = far(1)
    n0 = collect(0, m0)
    lo1 = low_x(1, lo1)
    m1 = near(1)
    k0 = near2(0)
    keep(1)
    m1 += relay(1, far1)
    lo1 = low_y(1, lo1)
    k0 += relay2(0, n0)
    finish(0, k0)
    low_z(1, lo1)
    n1 = collect(1, m1)
    k1 = near2(1)
    k1 += relay2(1, n1)
    finish(1, k1)
    for cp in sent:
        cp.wait_send()


def body(tokens, query_weight, down, up, request_combination, task_ids, coefficient):
    hbm = pl.BlockSpec(memory_space=pl.ANY)
    vmem = pl.BlockSpec(memory_space=pltpu.VMEM)
    n_sem = 160
    return pl.pallas_call(
        kernel,
        out_shape=jax.ShapeDtypeStruct((64, 2048), BF16),
        in_specs=[hbm, hbm, hbm, hbm, vmem, vmem, vmem],
        out_specs=vmem,
        scratch_shapes=[
            pltpu.VMEM((NS, 16, RS, 1024), BF16),
            pltpu.VMEM((1024, 2048), BF16),
            pltpu.VMEM((4, 8, 4096), BF16),
            pltpu.VMEM((2, 4, 4, 8, 1024), BF16),
            pltpu.VMEM((2, 4, 64, HALF), BF16),
            pltpu.VMEM((2, 4, 64, HALF), BF16),
            pltpu.VMEM((1024, 128), F32),
            pltpu.VMEM((1024, 128), F32),
            pltpu.VMEM((NS, 8, SR), F32),
            pltpu.VMEM((NS, 3, 8, SR), F32),
            pltpu.VMEM((NS, 3, 8, SR), F32),
            pltpu.VMEM((NS, 8, SR), F32),
            pltpu.VMEM((NS, 8, 8, SR), BF16),
            pltpu.VMEM((NS, 2, CR, HALF), BF16),
            pltpu.VMEM((NS, 2, 2, CR, QUART), BF16),
            pltpu.VMEM((NS, 2, 2, CR, HALF), BF16),
            pltpu.VMEM((NS, 2, 2, CR, HALF), BF16),
            pltpu.VMEM((NS, 2, CR, HALF), F32),
            pltpu.VMEM((NS, 2, RS, HALF), BF16),
            pltpu.VMEM((NS, 2, 2, RS, QUART), BF16),
            pltpu.VMEM((NS, 2, 2, RS, HALF), BF16),
            pltpu.VMEM((NS, 2, 2, RS, HALF), BF16),
            pltpu.SemaphoreType.DMA((n_sem,)),
            pltpu.SemaphoreType.DMA((n_sem,)),
            pltpu.SemaphoreType.DMA((16,)),
        ],
        compiler_params=pltpu.CompilerParams(
            collective_id=0, has_side_effects=True, vmem_limit_bytes=67043328
        ),
    )(
        tokens.reshape(2, 2, NS, RS, KC),
        query_weight,
        down.reshape(8, 8, 16384),
        up.reshape(64, 16384),
        request_combination.reshape(1, 2048),
        task_ids.T,
        coefficient.T,
    )


def solution(mesh):
    placed = (
        P("tensor", "adapter"),
        P("adapter", "tensor"),
        P("adapter", None, None),
        P("adapter", None, None),
        P(),
        P(),
        P(),
    )
    return jax.shard_map(
        body, mesh=mesh, in_specs=placed, out_specs=P("adapter", "tensor"), check_vma=False
    )
```

time: 241 us -> 70.4 us (0.29)
  waiting for transfers between devices: 161 us -> 0 us
  Pallas kernels: 0 us -> 68.4 us
  other arithmetic: 25.8 us -> 0 us
  starting transfers between devices: 16.1 us -> 0 us
  matrix products: 14.7 us -> 0 us
  between operations: 13.6 us -> 0.01 us
  local copies, waits for them, and re-layouts: 8.95 us -> 1.67 us
    reduce_scatter x1 -> x0, waiting for transfers between devices: 117 us -> none  [body(): lax.psum_scatter(jnp.dot(gathered, query_weight, preferred_element_type=j...]
    pallas_call x0 -> x1, Pallas kernels: none -> 68.4 us  [body(): pl.pallas_call(kernel, out_shape=jax.ShapeDtypeStruct((64, 2048), BF16),...]
    all_to_all x2 -> x0, waiting for transfers between devices: 43.1 us -> none  [the longest x1 29.7 us: body(): lax.all_to_all(delta_rows, 'tensor', split_axis=1, concat_axis=0, tiled=T...]
    scatter-add x1 -> x0, other arithmetic: 16.2 us -> none  [body(): delta_dense = jnp.zeros((total_rows, col_width), jnp.float32).at[row_targ...]
    all_to_all x2 -> x0, starting transfers between devices: 16.1 us -> none  [the longest x1 8.45 us: body(): lax.all_to_all(delta_rows, 'tensor', split_axis=1, concat_axis=0, tiled=T...]
    dot_general x3 -> x0, matrix products: 14.7 us -> none  [the longest x1 9.63 us: body(): jnp.dot(gathered, query_weight, preferred_element_type=jnp.float32)]
    another operation x2 -> x0, other arithmetic: 4.69 us -> none
    all_to_all x2 -> x0, local copies, waits for them, and re-layouts: 3.94 us -> none  [the longest x1 2.37 us: body(): lax.all_to_all(delta_rows, 'tensor', split_axis=1, concat_axis=0, tiled=T...]
  transfers between devices with their start and end apart: 4 -> 0, of which waited for: 3 -> 0; matrix products, arithmetic and copies ran while one was open for 9% -> 0% of each run, Pallas kernels for 0% -> 0%
where the time goes in v2:
time: 70.4 us; the launch traced here: 70.1 us
  Pallas kernels  68.4 us (97%)
  local copies, waits for them, and re-layouts  1.67 us (2%)
    pallas_call x1, Pallas kernels, body(): pl.pallas_call(kernel, out_shape=jax.ShapeDtypeStruct((64, 2048), BF16),...  68.4 us
    unnamed x1, local copies, waits for them, and re-layouts  1.67 us

profile of v2, /device:TPU:2, one launch (start us, length us, event | category | flops | bytes accessed | tf_op | source)
XLA Modules:
  0.0 70.1 jit_solution(14447712777184886303)
XLA Ops:
  0.0 68.4 %shard_map.73 = bf16[64,2048]{1,0:T(8,128)(2,1)} custom-call(bf16[2,2,2,32,512]{4,3,2,1,0:T(8,128)(2,1)} %bitcast.8, bf16[512,2048]{1,0:T(8,128)(2,1)} %w_hbm.1, bf16[8,8,16384]{2,1,0:T(8,128)(2,1)} %bitcast.6, bf16[64,16384]{1,0:T(8,128)(2,1)} %bitcast.7, s32[1,2048]{1,0:T(1,128)} %bitcast.9, s32[4,512]{1,0:T(4,128)} %bitcast.10, s32[4,512]{1,0:T(4,128)} %bitcast.11), custom_call_target="tpu_custom_call" | custom-call | tf_op jit(solution)/shard_map/pallas_call | solution.py:394
  68.4 1.7 %copy.9 = bf16[64,2048]{1,0:T(8,128)(2,1)} copy(bf16[64,2048]{1,0:T(8,128)(2,1)} %shard_map.73) | data formatting | bytes 524288

commit v3 on v2

v3 whole, which is shorter than its diff:
```python
import jax
import jax.numpy as jnp
from jax import lax
from jax.experimental import pallas as pl
from jax.experimental.pallas import tpu as pltpu
from jax.sharding import PartitionSpec as P

NS = 2
RS = 64 // NS
SR = 16 * RS
CR = 4 * RS
KC = 512
HALF = 1024
QUART = 512
TILE = 256
F32 = jnp.float32
BF16 = jnp.bfloat16


def kernel(
    tok_hbm, w_hbm, a_hbm, b_hbm, rows_ref, ids_ref, coef_ref,
    out_ref,
    tok, wf, a1, a2, bx, by,
    own_n, low_n, lt, lx, ly, low_own, low_all,
    s2, r2, s1, r1, acc, t2, q2, t1, q1,
    send_sem, recv_sem, local_sem,
):
    a_idx = lax.axis_index("adapter")
    z = lax.axis_index("tensor")
    x = a_idx // 8
    y = (a_idx // 2) % 4
    c = a_idx % 2
    other = 1 - c

    def dev(xx, yy, cc, zz):
        return {"adapter": (xx * 4 + yy) * 2 + cc, "tensor": zz}

    def x_peer(k):
        return dev((x + k) % 4, y, c, z)

    def y_peer(k):
        return dev(x, (y + k) % 4, c, z)

    def z_peer(k):
        return dev(x, y, c, (z + k) % 8)

    partner = dev(x, y, other, z)
    counter = [0, 0]
    sent = []

    def go(src, dst, device):
        i = counter[0]
        counter[0] += 1
        copy = pltpu.make_async_remote_copy(
            src, dst, send_sem.at[i], recv_sem.at[i],
            device_id=device, device_id_type=pl.DeviceIdType.MESH,
        )
        copy.start()
        sent.append(copy)
        return copy

    def local(src, dst):
        i = counter[1]
        counter[1] += 1
        copy = pltpu.make_async_copy(src, dst, local_sem.at[i])
        copy.start()
        return copy

    def arrived(copies):
        for cp in copies:
            cp.wait_recv()

    my_cols = pl.ds(pl.multiple_of(c * KC, KC), KC)
    tok_local = [
        local(tok_hbm.at[jj, c, s], tok.at[s, 2 * z + jj, :, my_cols])
        for s in range(NS) for jj in range(2)
    ]
    a_wide = lambda xx: pl.ds(pl.multiple_of(xx * 4096, 4096), 4096)
    a_narrow = lambda yy: pl.ds(pl.multiple_of(yy * 1024, 1024), 1024)
    a_local = local(a_hbm.at[z, :, a_wide(x)], a1.at[x])
    b_cols = [pl.ds(pl.multiple_of(z * 2048 + h * HALF, HALF), HALF) for h in range(2)]
    b_local = [
        local(b_hbm.at[:, b_cols[0]], bx.at[c, x]),
        local(b_hbm.at[:, b_cols[1]], by.at[c, y]),
    ]
    w_local = local(w_hbm, wf.at[my_cols, :])

    barrier = pltpu.get_barrier_semaphore()
    peers = [partner]
    peers += [x_peer(k) for k in range(1, 4)] + [y_peer(k) for k in range(1, 4)]
    peers += [z_peer(k) for k in range(1, 8)]
    for peer in peers:
        pl.semaphore_signal(barrier, inc=1, device_id=peer, device_id_type=pl.DeviceIdType.MESH)

    pl.semaphore_wait(barrier, len(peers))

    tok_pre = [
        go(tok_hbm.at[jj, other, s], tok.at[s, 2 * z + jj, :, my_cols], partner)
        for s in range(NS) for jj in range(2)
    ]
    a_x = [go(a_hbm.at[z, :, a_wide((x + k) % 4)], a1.at[x], x_peer(k)) for k in range(1, 4)]
    w_pre = go(w_hbm, wf.at[my_cols, :], partner)

    moving = {}

    def ring(s, k, u):
        ways = ("r", "l") if k < 3 else (("r",), ("l",))[u]
        for way in ways:
            if k > 0:
                moving.pop((s, k - 1, u, way)).wait_recv()
            b = (z - k + 8) % 8 if way == "r" else (z + k) % 8
            src = tok.at[s, 2 * b + u]
            moving[s, k, u, way] = go(src, src, z_peer(1 if way == "r" else 7))

    def ring_end(s):
        for key in [key for key in moving if key[0] == s]:
            moving.pop(key).wait_recv()

    def low_part(s):
        af = a2[...].reshape(256, 1024)
        for k in range(SR // TILE):
            nd = TILE // RS
            part = lax.dot_general(
                af, tok[s, nd * k:nd * (k + 1)].reshape(TILE, 1024),
                (((1,), (1,)), ((), ())), preferred_element_type=F32,
            )
            mine = owner[:, s * SR + TILE * k:s * SR + TILE * (k + 1)]
            total = jnp.zeros((8, TILE), F32)
            for g in range(32):
                o = ((g % 4) * 4 + (g // 4) % 4) * 2 + g // 16
                total += jnp.where(mine == o, part[8 * g:8 * (g + 1)], 0.0)
            lt[s, :, TILE * k:TILE * (k + 1)] = total
        return [go(lt.at[s], lx.at[s, k - 1], x_peer(k)) for k in range(1, 4)]

    def low_x(s, copies):
        arrived(copies)
        low_own[s] = (lt[s] + lx[s, 0]) + (lx[s, 1] + lx[s, 2])
        return [go(low_own.at[s], ly.at[s, k - 1], y_peer(k)) for k in range(1, 4)]

    def low_y(s, copies):
        arrived(copies)
        total = (low_own[s] + ly[s, 0]) + (ly[s, 1] + ly[s, 2])
        low_all[s, z] = (total * weight[:, s * SR:(s + 1) * SR]).astype(BF16)
        return [go(low_all.at[s, z], low_all.at[s, z], z_peer(k)) for k in (4, 3, 5, 2, 6, 1, 7)]

    def low_z(s, copies):
        arrived(copies)
        low_t = low_all[s].astype(F32).reshape(64, SR)
        for k in range(SR // 128):
            tile = low_t[:, 128 * k:128 * (k + 1)]
            low_n[s * SR + 128 * k:s * SR + 128 * (k + 1), :] = jnp.transpose(
                jnp.concatenate([tile, tile], axis=0)
            )

    place = (x, y)
    ring_peer = (x_peer, y_peer)

    def cut(n):
        return slice(n * TILE, (n + 1) * TILE)

    lo, hi = pl.ds(0, QUART), pl.ds(QUART, QUART)

    def dots(s, h, q, first, count, emit):
        if h == 0:
            lhs = tok[s, pl.ds(4 * q, 4)].reshape(CR, 1024)
        else:
            lhs = jnp.concatenate([tok[s, 4 * j + q] for j in range(4)], axis=0)
        for n in range(first, first + count):
            cols = slice(h * HALF + n * TILE, h * HALF + (n + 1) * TILE)
            emit(n, jnp.dot(lhs, wf[:, cols], preferred_element_type=F32))

    def far(s, hs=(0, 1)):
        out = []
        for h in hs:
            def put(n, v, h=h):
                s2[s, h, :, cut(n)] = v.astype(BF16)
            dots(s, h, (place[h] + 2) % 4, 0, 4, put)
            out.append(go(s2.at[s, h, :, lo], r2.at[s, h, 0], ring_peer[h](1)))
            out.append(go(s2.at[s, h, :, hi], r2.at[s, h, 1], ring_peer[h](3)))
        return out

    def near(s, hs=(0, 1)):
        out = []
        for h in hs:
            def put_r(n, v, h=h):
                s1[s, h, 0, :, cut(n)] = v.astype(BF16)
            def put_l(n, v, h=h):
                s1[s, h, 1, :, cut(n)] = v.astype(BF16)
            dots(s, h, (place[h] + 1) % 4, 2, 2, put_r)
            out.append(go(s1.at[s, h, 0, :, hi], r1.at[s, h, 0, :, hi], ring_peer[h](1)))
            dots(s, h, (place[h] + 3) % 4, 0, 2, put_l)
            out.append(go(s1.at[s, h, 1, :, lo], r1.at[s, h, 1, :, lo], ring_peer[h](3)))
        return out

    def keep(s):
        for h in range(2):
            def put(n, v, h=h):
                acc[s, h, :, cut(n)] = v
            dots(s, h, place[h], 0, 4, put)

    def relay(s, copies, hs=(0, 1)):
        out = []
        for h in hs:
            arrived(copies[2 * h:2 * h + 2])
            def add_r(n, v, h=h):
                s1[s, h, 0, :, cut(n)] = (v + r2[s, h, 0, :, cut(n)].astype(F32)).astype(BF16)
            def add_l(n, v, h=h):
                s1[s, h, 1, :, cut(n)] = (v + r2[s, h, 1, :, cut(n - 2)].astype(F32)).astype(BF16)
            dots(s, h, (place[h] + 1) % 4, 0, 2, add_r)
            out.append(go(s1.at[s, h, 0, :, lo], r1.at[s, h, 0, :, lo], ring_peer[h](1)))
            dots(s, h, (place[h] + 3) % 4, 2, 2, add_l)
            out.append(go(s1.at[s, h, 1, :, hi], r1.at[s, h, 1, :, hi], ring_peer[h](3)))
        return out

    lane = lax.broadcasted_iota(jnp.int32, (CR, 128), 1)

    def masked(s, h):
        if h == 0:
            at = pl.ds(pl.multiple_of(s * SR + x * CR, CR), CR)
            ow, lw = own_n[at, :], low_n[at, :]
        else:
            ats = [pl.ds(pl.multiple_of(s * SR + (4 * j + y) * RS, RS), RS) for j in range(4)]
            ow = jnp.concatenate([own_n[at, :] for at in ats], axis=0)
            lw = jnp.concatenate([low_n[at, :] for at in ats], axis=0)
        pieces = []
        for cc in range(2):
            for m in range(2):
                if h == 0:
                    o0, step = ((2 * m) * 4 + y) * 2 + cc, 8
                else:
                    o0, step = (x * 4 + 2 * m) * 2 + cc, 2
                want = jnp.where(lane < 64, o0, o0 + step).astype(F32)
                pieces.append(jnp.where(ow == want, lw, 0.0).astype(BF16))
        return jnp.concatenate(pieces, axis=1)

    place2 = (y, x)
    peer2 = (y_peer, x_peer)

    def block(h, q):
        return pl.ds(pl.multiple_of(q * RS, RS), RS)

    def collect(s, copies):
        arrived(copies)
        out = []
        for h in range(2):
            lhs = masked(s, h)
            up = (bx, by)[h]
            for n in range(4):
                delta = jnp.dot(
                    lhs, up[:, :, :, cut(n)].reshape(512, TILE), preferred_element_type=F32
                )
                acc[s, h, :, cut(n)] = (acc[s, h, :, cut(n)] + delta) + (
                    r1[s, h, 0, :, cut(n)].astype(F32) + r1[s, h, 1, :, cut(n)].astype(F32)
                )
            t2[s, h] = acc[s, h, block(h, (place2[h] + 2) % 4), :].astype(BF16)
            out.append(go(t2.at[s, h, :, lo], q2.at[s, h, 0], peer2[h](1)))
            out.append(go(t2.at[s, h, :, hi], q2.at[s, h, 1], peer2[h](3)))
        return out

    def near2(s):
        out = []
        for h in range(2):
            t1[s, h, 0, :, QUART:] = acc[s, h, block(h, (place2[h] + 1) % 4), QUART:].astype(BF16)
            out.append(go(t1.at[s, h, 0, :, hi], q1.at[s, h, 0, :, hi], peer2[h](1)))
            t1[s, h, 1, :, :QUART] = acc[s, h, block(h, (place2[h] + 3) % 4), :QUART].astype(BF16)
            out.append(go(t1.at[s, h, 1, :, lo], q1.at[s, h, 1, :, lo], peer2[h](3)))
        return out

    def relay2(s, copies):
        out = []
        for h in range(2):
            arrived(copies[2 * h:2 * h + 2])
            t1[s, h, 0, :, :QUART] = (
                acc[s, h, block(h, (place2[h] + 1) % 4), :QUART] + q2[s, h, 0].astype(F32)
            ).astype(BF16)
            out.append(go(t1.at[s, h, 0, :, lo], q1.at[s, h, 0, :, lo], peer2[h](1)))
            t1[s, h, 1, :, QUART:] = (
                acc[s, h, block(h, (place2[h] + 3) % 4), QUART:] + q2[s, h, 1].astype(F32)
            ).astype(BF16)
            out.append(go(t1.at[s, h, 1, :, hi], q1.at[s, h, 1, :, hi], peer2[h](3)))
        return out

    def finish(s, copies):
        arrived(copies)
        for h in range(2):
            out_ref[s * RS:(s + 1) * RS, h * HALF:(h + 1) * HALF] = (
                acc[s, h, block(h, place2[h]), :]
                + (q1[s, h, 0].astype(F32) + q1[s, h, 1].astype(F32))
            ).astype(BF16)

    for cp in tok_local:
        cp.wait()
    arrived(tok_pre[:1])
    ring(0, 0, 0)
    lane8 = lax.broadcasted_iota(jnp.int32, (8, 128), 1)
    per = 128 // RS
    groups = []
    for s in range(NS):
        for g in range(16 // per):
            piece = jnp.zeros((8, 128), jnp.int32)
            for j in range(per):
                d = per * g + j
                raw = jnp.broadcast_to(rows_ref[:, 128 * d:128 * (d + 1)], (8, 128))
                shift = (RS * j - RS * s + 256 - 64 * c) % 128
                piece = jnp.where(lane8 // RS == j, pltpu.roll(raw, shift, 1), piece)
            groups.append(piece[0:1])

    combo = lax.broadcasted_iota(jnp.int32, (4, 512), 1)
    hit = (ids_ref[...] - (combo // 16) * 4) == (z // 2)
    table = 0.25 * jnp.sum(jnp.where(hit, coef_ref[...], 0).astype(F32), axis=0, keepdims=True)
    column = jnp.concatenate(
        [
            jnp.transpose(jnp.broadcast_to(table[:, 128 * k:128 * (k + 1)], (128, 128)))
            for k in range(4)
        ],
        axis=0,
    )
    number = lax.broadcasted_iota(jnp.int32, (512, 128), 0)
    weight = jnp.concatenate(
        [
            jnp.sum(jnp.where(number == g, column, 0.0), axis=0, keepdims=True)
            for g in groups
        ],
        axis=1,
    )
    rows = jnp.concatenate(groups, axis=1)
    owner = rows // 16
    arrived(tok_pre[1:2])
    ring(0, 0, 1)
    owner_f = owner.astype(F32)
    for k in range(8):
        tile = jnp.broadcast_to(owner_f[:, 128 * k:128 * (k + 1)], (128, 128))
        own_n[128 * k:128 * (k + 1), :] = jnp.transpose(tile)

    a_local.wait()
    arrived(tok_pre[2:])
    ring(0, 1, 0)
    ring(0, 1, 1)
    arrived(a_x)
    a_own = local(a1.at[:, :, a_narrow(y)], a2.at[c, y])
    a_y = [go(a1.at[:, :, a_narrow((y + k) % 4)], a2.at[c, y], y_peer(k)) for k in range(1, 4)]
    b_x = [go(b_hbm.at[:, b_cols[0]], bx.at[c, x], x_peer(k)) for k in range(1, 4)]
    b_y = [go(b_hbm.at[:, b_cols[1]], by.at[c, y], y_peer(k)) for k in range(1, 4)]
    ring(0, 2, 0)
    ring(0, 2, 1)
    a_own.wait()
    for cp in b_local:
        cp.wait()
    w_local.wait()
    ring(0, 3, 0)
    ring(1, 0, 0)
    ring(0, 3, 1)
    ring(1, 0, 1)
    arrived(a_y)
    a_c = go(a2.at[c], a2.at[c], partner)
    arrived([w_pre])
    ring_end(0)

    far0 = far(0, (0,))
    ring(1, 1, 0)
    far0 += far(0, (1,))
    ring(1, 1, 1)
    arrived([a_c])
    lo0 = low_part(0)
    m0 = near(0, (0,))
    ring(1, 2, 0)
    m0 += near(0, (1,))
    keep(0)
    ring(1, 2, 1)
    arrived(b_x + b_y)
    b_c = [go(bx.at[c], bx.at[c], partner), go(by.at[c], by.at[c], partner)]
    lo0 = low_x(0, lo0)
    ring(1, 3, 0)
    m0 += relay(0, far0)
    ring(1, 3, 1)
    ring_end(1)

    lo1 = low_part(1)
    far1 = far(1)
    lo0 = low_y(0, lo0)
    m1 = near(1)
    keep(1)
    lo1 = low_x(1, lo1)
    arrived(b_c)
    low_z(0, lo0)
    n0 = collect(0, m0)
    k0 = near2(0)
    lo1 = low_y(1, lo1)
    m1 += relay(1, far1)
    k0 += relay2(0, n0)
    finish(0, k0)
    low_z(1, lo1)
    n1 = collect(1, m1)
    k1 = near2(1)
    k1 += relay2(1, n1)
    finish(1, k1)
    for cp in sent:
        cp.wait_send()


def body(tokens, query_weight, down, up, request_combination, task_ids, coefficient):
    hbm = pl.BlockSpec(memory_space=pl.ANY)
    vmem = pl.BlockSpec(memory_space=pltpu.VMEM)
    n_sem = 160
    return pl.pallas_call(
        kernel,
        out_shape=jax.ShapeDtypeStruct((64, 2048), BF16),
        in_specs=[hbm, hbm, hbm, hbm, vmem, vmem, vmem],
        out_specs=vmem,
        scratch_shapes=[
            pltpu.VMEM((NS, 16, RS, 1024), BF16),
            pltpu.VMEM((1024, 2048), BF16),
            pltpu.VMEM((4, 8, 4096), BF16),
            pltpu.VMEM((2, 4, 4, 8, 1024), BF16),
            pltpu.VMEM((2, 4, 64, HALF), BF16),
            pltpu.VMEM((2, 4, 64, HALF), BF16),
            pltpu.VMEM((1024, 128), F32),
            pltpu.VMEM((1024, 128), F32),
            pltpu.VMEM((NS, 8, SR), F32),
            pltpu.VMEM((NS, 3, 8, SR), F32),
            pltpu.VMEM((NS, 3, 8, SR), F32),
            pltpu.VMEM((NS, 8, SR), F32),
            pltpu.VMEM((NS, 8, 8, SR), BF16),
            pltpu.VMEM((NS, 2, CR, HALF), BF16),
            pltpu.VMEM((NS, 2, 2, CR, QUART), BF16),
            pltpu.VMEM((NS, 2, 2, CR, HALF), BF16),
            pltpu.VMEM((NS, 2, 2, CR, HALF), BF16),
            pltpu.VMEM((NS, 2, CR, HALF), F32),
            pltpu.VMEM((NS, 2, RS, HALF), BF16),
            pltpu.VMEM((NS, 2, 2, RS, QUART), BF16),
            pltpu.VMEM((NS, 2, 2, RS, HALF), BF16),
            pltpu.VMEM((NS, 2, 2, RS, HALF), BF16),
            pltpu.SemaphoreType.DMA((n_sem,)),
            pltpu.SemaphoreType.DMA((n_sem,)),
            pltpu.SemaphoreType.DMA((16,)),
        ],
        compiler_params=pltpu.CompilerParams(
            collective_id=0, has_side_effects=True, vmem_limit_bytes=67043328
        ),
    )(
        tokens.reshape(2, 2, NS, RS, KC),
        query_weight,
        down.reshape(8, 8, 16384),
        up.reshape(64, 16384),
        request_combination.reshape(1, 2048),
        task_ids.T,
        coefficient.T,
    )


def solution(mesh):
    placed = (
        P("tensor", "adapter"),
        P("adapter", "tensor"),
        P("adapter", None, None),
        P("adapter", None, None),
        P(),
        P(),
        P(),
    )
    return jax.shard_map(
        body, mesh=mesh, in_specs=placed, out_specs=P("adapter", "tensor"), check_vma=False
    )
```

time: 70.4 us -> 70.8 us (level)
  no operation moved by 1% of the time
where the time goes in v3:
time: 70.8 us; the launch traced here: 69.9 us
  Pallas kernels  68.2 us (96%)
  local copies, waits for them, and re-layouts  1.67 us (2%)
    pallas_call x1, Pallas kernels, body(): pl.pallas_call(kernel, out_shape=jax.ShapeDtypeStruct((64, 2048), BF16),...  68.2 us
    unnamed x1, local copies, waits for them, and re-layouts  1.67 us

profile of v3, /device:TPU:2, one launch (start us, length us, event | category | flops | bytes accessed | tf_op | source)
XLA Modules:
  0.0 69.9 jit_solution(9238423118942098812)
XLA Ops:
  0.0 68.2 %shard_map.73 = bf16[64,2048]{1,0:T(8,128)(2,1)} custom-call(bf16[2,2,2,32,512]{4,3,2,1,0:T(8,128)(2,1)} %bitcast.8, bf16[512,2048]{1,0:T(8,128)(2,1)} %w_hbm.1, bf16[8,8,16384]{2,1,0:T(8,128)(2,1)} %bitcast.6, bf16[64,16384]{1,0:T(8,128)(2,1)} %bitcast.7, s32[1,2048]{1,0:T(1,128)} %bitcast.9, s32[4,512]{1,0:T(4,128)} %bitcast.10, s32[4,512]{1,0:T(4,128)} %bitcast.11), custom_call_target="tpu_custom_call" | custom-call | tf_op jit(solution)/shard_map/pallas_call | solution.py:405
  68.2 1.7 %copy.9 = bf16[64,2048]{1,0:T(8,128)(2,1)} copy(bf16[64,2048]{1,0:T(8,128)(2,1)} %shard_map.73) | data formatting | bytes 524288

commit v4 on v3

--- a/solution.py
+++ b/solution.py
@@ -5,7 +5,7 @@
 from jax.experimental.pallas import tpu as pltpu
 from jax.sharding import PartitionSpec as P
 
-NS = 2
+NS = 4
 RS = 64 // NS
 SR = 16 * RS
 CR = 4 * RS
@@ -22,7 +22,7 @@
     out_ref,
     tok, wf, a1, a2, bx, by,
     own_n, low_n, lt, lx, ly, low_own, low_all,
-    s2, r2, s1, r1, acc, t2, q2, t1, q1,
+    s2, r2, s1, r1, acc, t1, q1,
     send_sem, recv_sem, local_sem,
 ):
     a_idx = lax.axis_index("adapter")
@@ -192,8 +192,8 @@
             out.append(go(s1.at[s, h, 1, :, lo], r1.at[s, h, 1, :, lo], ring_peer[h](3)))
         return out
 
-    def keep(s):
-        for h in range(2):
+    def keep(s, hs=(0, 1)):
+        for h in hs:
             def put(n, v, h=h):
                 acc[s, h, :, cut(n)] = v
             dots(s, h, place[h], 0, 4, put)
@@ -201,7 +201,7 @@
     def relay(s, copies, hs=(0, 1)):
         out = []
         for h in hs:
-            arrived(copies[2 * h:2 * h + 2])
+            arrived(copies)
             def add_r(n, v, h=h):
                 s1[s, h, 0, :, cut(n)] = (v + r2[s, h, 0, :, cut(n)].astype(F32)).astype(BF16)
             def add_l(n, v, h=h):
@@ -239,58 +239,34 @@
     def block(h, q):
         return pl.ds(pl.multiple_of(q * RS, RS), RS)
 
-    def collect(s, copies):
+    def collect(s, h, copies):
         arrived(copies)
+        lhs = masked(s, h)
+        up = (bx, by)[h]
+        for n in range(4):
+            delta = jnp.dot(
+                lhs, up[:, :, :, cut(n)].reshape(512, TILE), preferred_element_type=F32
+            )
+            acc[s, h, :, cut(n)] = (acc[s, h, :, cut(n)] + delta) + (
+                r1[s, h, 0, :, cut(n)].astype(F32) + r1[s, h, 1, :, cut(n)].astype(F32)
+            )
         out = []
-        for h in range(2):
-            lhs = masked(s, h)
-            up = (bx, by)[h]
-            for n in range(4):
-                delta = jnp.dot(
-                    lhs, up[:, :, :, cut(n)].reshape(512, TILE), preferred_element_type=F32
-                )
-                acc[s, h, :, cut(n)] = (acc[s, h, :, cut(n)] + delta) + (
-                    r1[s, h, 0, :, cut(n)].astype(F32) + r1[s, h, 1, :, cut(n)].astype(F32)
-                )
-            t2[s, h] = acc[s, h, block(h, (place2[h] + 2) % 4), :].astype(BF16)
-            out.append(go(t2.at[s, h, :, lo], q2.at[s, h, 0], peer2[h](1)))
-            out.append(go(t2.at[s, h, :, hi], q2.at[s, h, 1], peer2[h](3)))
+        for k in (2, 1, 3):
+            t1[s, h, k - 1] = acc[s, h, block(h, (place2[h] + k) % 4), :].astype(BF16)
+            out.append(go(t1.at[s, h, k - 1], q1.at[s, h, k - 1], peer2[h](k)))
         return out
 
-    def near2(s):
-        out = []
-        for h in range(2):
-            t1[s, h, 0, :, QUART:] = acc[s, h, block(h, (place2[h] + 1) % 4), QUART:].astype(BF16)
-            out.append(go(t1.at[s, h, 0, :, hi], q1.at[s, h, 0, :, hi], peer2[h](1)))
-            t1[s, h, 1, :, :QUART] = acc[s, h, block(h, (place2[h] + 3) % 4), :QUART].astype(BF16)
-            out.append(go(t1.at[s, h, 1, :, lo], q1.at[s, h, 1, :, lo], peer2[h](3)))
-        return out
-
-    def relay2(s, copies):
-        out = []
-        for h in range(2):
-            arrived(copies[2 * h:2 * h + 2])
-            t1[s, h, 0, :, :QUART] = (
-                acc[s, h, block(h, (place2[h] + 1) % 4), :QUART] + q2[s, h, 0].astype(F32)
-            ).astype(BF16)
-            out.append(go(t1.at[s, h, 0, :, lo], q1.at[s, h, 0, :, lo], peer2[h](1)))
-            t1[s, h, 1, :, QUART:] = (
-                acc[s, h, block(h, (place2[h] + 3) % 4), QUART:] + q2[s, h, 1].astype(F32)
-            ).astype(BF16)
-            out.append(go(t1.at[s, h, 1, :, hi], q1.at[s, h, 1, :, hi], peer2[h](3)))
-        return out
-
-    def finish(s, copies):
+    def finish(s, h, copies):
         arrived(copies)
-        for h in range(2):
-            out_ref[s * RS:(s + 1) * RS, h * HALF:(h + 1) * HALF] = (
-                acc[s, h, block(h, place2[h]), :]
-                + (q1[s, h, 0].astype(F32) + q1[s, h, 1].astype(F32))
-            ).astype(BF16)
-
+        out_ref[s * RS:(s + 1) * RS, h * HALF:(h + 1) * HALF] = (
+            (acc[s, h, block(h, place2[h]), :] + q1[s, h, 0].astype(F32))
+            + (q1[s, h, 1].astype(F32) + q1[s, h, 2].astype(F32))
+        ).astype(BF16)
+
+    lows, fars, mids, ends = {}, {}, {}, {}
     for cp in tok_local:
         cp.wait()
-    arrived(tok_pre[:1])
+    arrived(tok_pre[0:1])
     ring(0, 0, 0)
     lane8 = lax.broadcasted_iota(jnp.int32, (8, 128), 1)
     per = 128 // RS
@@ -327,73 +303,132 @@
     owner = rows // 16
     arrived(tok_pre[1:2])
     ring(0, 0, 1)
+    arrived(tok_pre[2:3])
+    ring(1, 0, 0)
+    arrived(tok_pre[3:4])
+    ring(1, 0, 1)
     owner_f = owner.astype(F32)
     for k in range(8):
         tile = jnp.broadcast_to(owner_f[:, 128 * k:128 * (k + 1)], (128, 128))
         own_n[128 * k:128 * (k + 1), :] = jnp.transpose(tile)
 
-    a_local.wait()
-    arrived(tok_pre[2:])
     ring(0, 1, 0)
     ring(0, 1, 1)
+    a_local.wait()
     arrived(a_x)
     a_own = local(a1.at[:, :, a_narrow(y)], a2.at[c, y])
     a_y = [go(a1.at[:, :, a_narrow((y + k) % 4)], a2.at[c, y], y_peer(k)) for k in range(1, 4)]
     b_x = [go(b_hbm.at[:, b_cols[0]], bx.at[c, x], x_peer(k)) for k in range(1, 4)]
     b_y = [go(b_hbm.at[:, b_cols[1]], by.at[c, y], y_peer(k)) for k in range(1, 4)]
+    ring(1, 1, 0)
+    ring(1, 1, 1)
     ring(0, 2, 0)
+    arrived(tok_pre[4:5])
+    ring(2, 0, 0)
     ring(0, 2, 1)
+    arrived(tok_pre[5:6])
+    ring(2, 0, 1)
+    ring(1, 2, 0)
+    arrived(tok_pre[6:7])
+    ring(3, 0, 0)
+    ring(1, 2, 1)
+    arrived(tok_pre[7:8])
+    ring(3, 0, 1)
+    ring(0, 3, 0)
+    ring(2, 1, 0)
     a_own.wait()
+    arrived(a_y)
+    a_c = go(a2.at[c], a2.at[c], partner)
+    ring(0, 3, 1)
+    ring(2, 1, 1)
+    ring(1, 3, 0)
+    ring(3, 1, 0)
+    ring(1, 3, 1)
+    ring(3, 1, 1)
+    ring(2, 2, 0)
+    arrived([a_c])
+    ring_end(0)
+    lows[0] = low_part(0)
+    w_local.wait()
+    arrived([w_pre])
+    fars[0, 1] = far(0, (1,))
+    fars[0, 0] = far(0, (0,))
+    mids[0, 1] = near(0, (1,))
+    ring(2, 2, 1)
+    mids[0, 0] = near(0, (0,))
     for cp in b_local:
         cp.wait()
-    w_local.wait()
-    ring(0, 3, 0)
-    ring(1, 0, 0)
-    ring(0, 3, 1)
-    ring(1, 0, 1)
-    arrived(a_y)
-    a_c = go(a2.at[c], a2.at[c], partner)
-    arrived([w_pre])
-    ring_end(0)
-
-    far0 = far(0, (0,))
-    ring(1, 1, 0)
-    far0 += far(0, (1,))
-    ring(1, 1, 1)
-    arrived([a_c])
-    lo0 = low_part(0)
-    m0 = near(0, (0,))
-    ring(1, 2, 0)
-    m0 += near(0, (1,))
-    keep(0)
-    ring(1, 2, 1)
     arrived(b_x + b_y)
     b_c = [go(bx.at[c], bx.at[c], partner), go(by.at[c], by.at[c], partner)]
-    lo0 = low_x(0, lo0)
-    ring(1, 3, 0)
-    m0 += relay(0, far0)
-    ring(1, 3, 1)
+    keep(0, (0,))
+    keep(0, (1,))
+    ring(3, 2, 0)
     ring_end(1)
-
-    lo1 = low_part(1)
-    far1 = far(1)
-    lo0 = low_y(0, lo0)
-    m1 = near(1)
-    keep(1)
-    lo1 = low_x(1, lo1)
+    lows[1] = low_part(1)
+    fars[1, 1] = far(1, (1,))
+    fars[1, 0] = far(1, (0,))
+    mids[1, 0] = near(1, (0,))
+    ring(3, 2, 1)
+    mids[1, 1] = near(1, (1,))
+    keep(1, (1,))
+    keep(1, (0,))
+    ring(2, 3, 0)
+    lows[0] = low_x(0, lows[0])
+    ring(2, 3, 1)
+    mids[0, 1] += relay(0, fars[0, 1], (1,))
+    mids[0, 0] += relay(0, fars[0, 0], (0,))
+    ring(3, 3, 0)
+    ring(3, 3, 1)
+    lows[1] = low_x(1, lows[1])
+    ring_end(2)
+    lows[2] = low_part(2)
+    mids[1, 1] += relay(1, fars[1, 1], (1,))
+    mids[1, 0] += relay(1, fars[1, 0], (0,))
+    fars[2, 0] = far(2, (0,))
+    fars[2, 1] = far(2, (1,))
+    mids[2, 0] = near(2, (0,))
+    mids[2, 1] = near(2, (1,))
+    keep(2, (1,))
+    keep(2, (0,))
+    ring_end(3)
+    lows[3] = low_part(3)
+    fars[3, 1] = far(3, (1,))
+    fars[3, 0] = far(3, (0,))
+    mids[3, 0] = near(3, (0,))
+    lows[0] = low_y(0, lows[0])
+    mids[3, 1] = near(3, (1,))
+    keep(3, (0,))
+    keep(3, (1,))
+    lows[1] = low_y(1, lows[1])
+    lows[2] = low_x(2, lows[2])
+    mids[2, 1] += relay(2, fars[2, 1], (1,))
+    mids[2, 0] += relay(2, fars[2, 0], (0,))
+    low_z(0, lows[0])
     arrived(b_c)
-    low_z(0, lo0)
-    n0 = collect(0, m0)
-    k0 = near2(0)
-    lo1 = low_y(1, lo1)
-    m1 += relay(1, far1)
-    k0 += relay2(0, n0)
-    finish(0, k0)
-    low_z(1, lo1)
-    n1 = collect(1, m1)
-    k1 = near2(1)
-    k1 += relay2(1, n1)
-    finish(1, k1)
+    ends[0, 0] = collect(0, 0, mids[0, 0])
+    lows[3] = low_x(3, lows[3])
+    ends[0, 1] = collect(0, 1, mids[0, 1])
+    mids[3, 0] += relay(3, fars[3, 0], (0,))
+    mids[3, 1] += relay(3, fars[3, 1], (1,))
+    low_z(1, lows[1])
+    ends[1, 1] = collect(1, 1, mids[1, 1])
+    ends[1, 0] = collect(1, 0, mids[1, 0])
+    lows[2] = low_y(2, lows[2])
+    finish(0, 0, ends[0, 0])
+    finish(0, 1, ends[0, 1])
+    lows[3] = low_y(3, lows[3])
+    low_z(2, lows[2])
+    ends[2, 1] = collect(2, 1, mids[2, 1])
+    ends[2, 0] = collect(2, 0, mids[2, 0])
+    finish(1, 0, ends[1, 0])
+    finish(1, 1, ends[1, 1])
+    low_z(3, lows[3])
+    ends[3, 1] = collect(3, 1, mids[3, 1])
+    ends[3, 0] = collect(3, 0, mids[3, 0])
+    finish(2, 1, ends[2, 1])
+    finish(2, 0, ends[2, 0])
+    finish(3, 1, ends[3, 1])
+    finish(3, 0, ends[3, 0])
     for cp in sent:
         cp.wait_send()
 
@@ -401,7 +436,7 @@
 def body(tokens, query_weight, down, up, request_combination, task_ids, coefficient):
     hbm = pl.BlockSpec(memory_space=pl.ANY)
     vmem = pl.BlockSpec(memory_space=pltpu.VMEM)
-    n_sem = 160
+    n_sem = 256
     return pl.pallas_call(
         kernel,
         out_shape=jax.ShapeDtypeStruct((64, 2048), BF16),
@@ -426,10 +461,8 @@
             pltpu.VMEM((NS, 2, 2, CR, HALF), BF16),
             pltpu.VMEM((NS, 2, 2, CR, HALF), BF16),
             pltpu.VMEM((NS, 2, CR, HALF), F32),
-            pltpu.VMEM((NS, 2, RS, HALF), BF16),
-            pltpu.VMEM((NS, 2, 2, RS, QUART), BF16),
-            pltpu.VMEM((NS, 2, 2, RS, HALF), BF16),
-            pltpu.VMEM((NS, 2, 2, RS, HALF), BF16),
+            pltpu.VMEM((NS, 2, 3, RS, HALF), BF16),
+            pltpu.VMEM((NS, 2, 3, RS, HALF), BF16),
             pltpu.SemaphoreType.DMA((n_sem,)),
             pltpu.SemaphoreType.DMA((n_sem,)),
             pltpu.SemaphoreType.DMA((16,)),

time: 70.8 us -> 70.3 us (level); the launches traced: 69.9 us -> 70.1 us
  no operation moved by 1% of the time
where the time goes in v4:
time: 70.3 us; the launch traced here: 70.1 us
  Pallas kernels  68.5 us (97%)
  local copies, waits for them, and re-layouts  1.67 us (2%)
    pallas_call x1, Pallas kernels, body(): pl.pallas_call(kernel, out_shape=jax.ShapeDtypeStruct((64, 2048), BF16),...  68.5 us
    unnamed x1, local copies, waits for them, and re-layouts  1.67 us

profile of v4, /device:TPU:2, one launch (start us, length us, event | category | flops | bytes accessed | tf_op | source)
XLA Modules:
  0.0 70.1 jit_solution(17410831063045208136)
XLA Ops:
  0.0 68.5 %shard_map.73 = bf16[64,2048]{1,0:T(8,128)(2,1)} custom-call(bf16[2,2,4,16,512]{4,3,2,1,0:T(8,128)(2,1)} %bitcast.8, bf16[512,2048]{1,0:T(8,128)(2,1)} %w_hbm.1, bf16[8,8,16384]{2,1,0:T(8,128)(2,1)} %bitcast.6, bf16[64,16384]{1,0:T(8,128)(2,1)} %bitcast.7, s32[1,2048]{1,0:T(1,128)} %bitcast.9, s32[4,512]{1,0:T(4,128)} %bitcast.10, s32[4,512]{1,0:T(4,128)} %bitcast.11), custom_call_target="tpu_custom_call" | custom-call | tf_op jit(solution)/shard_map/pallas_call | solution.py:440
  68.5 1.7 %copy.9 = bf16[64,2048]{1,0:T(8,128)(2,1)} copy(bf16[64,2048]{1,0:T(8,128)(2,1)} %shard_map.73) | data formatting | bytes 524288

commit v5 on v4

v5 whole, which is shorter than its diff:
```python
import math

import jax
import jax.numpy as jnp
from jax import lax
from jax.experimental import pallas as pl
from jax.experimental.pallas import tpu as pltpu
from jax.sharding import PartitionSpec as P

NS = 4
RS = 64 // NS
SR = 16 * RS
CR = 4 * RS
KC = 512
HALF = 1024
QUART = 512
TILE = 256
F32 = jnp.float32
BF16 = jnp.bfloat16


def kernel(
    tok_hbm, w_hbm, a_hbm, b_hbm, rows_ref, ids_ref, coef_ref,
    out_ref,
    tok, wf, a1, a2, bx, by,
    own_n, low_n, lt, lx, ly, low_own, low_all,
    s2, r2, s1, r1, acc, t1, q1,
    send_sem, recv_sem, local_sem,
):
    a_idx = lax.axis_index("adapter")
    z = lax.axis_index("tensor")
    x = a_idx // 8
    y = (a_idx // 2) % 4
    c = a_idx % 2
    other = 1 - c

    def dev(xx, yy, cc, zz):
        return {"adapter": (xx * 4 + yy) * 2 + cc, "tensor": zz}

    def x_peer(k):
        return dev((x + k) % 4, y, c, z)

    def y_peer(k):
        return dev(x, (y + k) % 4, c, z)

    def z_peer(k):
        return dev(x, y, c, (z + k) % 8)

    partner = dev(x, y, other, z)
    counter = [0, 0]
    sent = [0] * 5
    START, UP, RING, SUMS, LOWS = range(5)

    def arrival():
        counter[0] += 1
        return counter[0] - 1

    def go(src, dst, device, mark, group):
        pltpu.make_async_remote_copy(
            src, dst, send_sem.at[group], recv_sem.at[mark],
            device_id=device, device_id_type=pl.DeviceIdType.MESH,
        ).start()
        sent[group] += math.prod(src.shape) * src.dtype.itemsize

    def arrived(mark, ref):
        pltpu.make_async_remote_copy(
            ref, ref, send_sem.at[0], recv_sem.at[mark],
            device_id=partner, device_id_type=pl.DeviceIdType.MESH,
        ).wait_recv()

    def gone(group, ref):
        row = math.prod(ref.shape[1:]) * ref.dtype.itemsize
        part = ref.at[pl.ds(0, sent[group] // row)]
        pltpu.make_async_remote_copy(
            part, part, send_sem.at[group], recv_sem.at[0],
            device_id=partner, device_id_type=pl.DeviceIdType.MESH,
        ).wait_send()

    def local(src, dst):
        i = counter[1]
        counter[1] += 1
        copy = pltpu.make_async_copy(src, dst, local_sem.at[i])
        copy.start()
        return copy

    my_cols = pl.ds(pl.multiple_of(c * KC, KC), KC)
    tok_local = [
        local(tok_hbm.at[:, c, s], tok.at[s, c, pl.ds(2 * z, 2)]) for s in range(NS)
    ]
    a_wide = lambda xx: pl.ds(pl.multiple_of(xx * 4096, 4096), 4096)
    a_narrow = lambda yy: pl.ds(pl.multiple_of(yy * 1024, 1024), 1024)
    a_local = local(a_hbm.at[z, :, a_wide(x)], a1.at[x])
    b_cols = [pl.ds(pl.multiple_of(z * 2048 + h * HALF, HALF), HALF) for h in range(2)]
    b_local = [
        local(b_hbm.at[:, b_cols[0]], bx.at[c, x]),
        local(b_hbm.at[:, b_cols[1]], by.at[c, y]),
    ]
    w_local = local(w_hbm, wf.at[my_cols, :])

    barrier = pltpu.get_barrier_semaphore()
    peers = [partner]
    peers += [x_peer(k) for k in range(1, 4)] + [y_peer(k) for k in range(1, 4)]
    peers += [z_peer(k) for k in range(1, 8)]
    for peer in peers:
        pl.semaphore_signal(barrier, inc=1, device_id=peer, device_id_type=pl.DeviceIdType.MESH)

    pl.semaphore_wait(barrier, len(peers))

    tok_pre = [arrival() for _ in range(NS)]

    def exchange(s):
        go(tok_hbm.at[:, other, s], tok.at[s, c, pl.ds(2 * z, 2)], partner, tok_pre[s], START)

    a_x, w_pre, a_y, a_c, b_x, b_y, b_c = [arrival() for _ in range(7)]

    moving = {}

    def ring(s, k, u):
        half = c if u == 0 else other
        if k > 0:
            arrived(moving.pop((s, k - 1, u)), tok.at[s, 0, pl.ds(0, 4)])
        moving[s, k, u] = mark = arrival()
        if k < 3 or u == 0:
            src = tok.at[s, half, pl.ds(2 * ((z - k + 8) % 8), 2)]
            go(src, src, z_peer(1), mark, RING)
        if k < 3 or u == 1:
            src = tok.at[s, half, pl.ds(2 * ((z + k) % 8), 2)]
            go(src, src, z_peer(7), mark, RING)

    def ring_end(s):
        for u in range(2):
            arrived(moving.pop((s, 3, u)), tok.at[s, 0, pl.ds(0, 2)])

    def wide(halves):
        return jnp.concatenate(halves, axis=1)

    def low_part(s):
        af = a2[...].reshape(256, 1024)
        for k in range(SR // TILE):
            nd = TILE // RS
            part = lax.dot_general(
                af, wide([tok[s, kc, nd * k:nd * (k + 1)].reshape(TILE, KC) for kc in range(2)]),
                (((1,), (1,)), ((), ())), preferred_element_type=F32,
            )
            mine = owner[:, s * SR + TILE * k:s * SR + TILE * (k + 1)]
            total = jnp.zeros((8, TILE), F32)
            for g in range(32):
                o = ((g % 4) * 4 + (g // 4) % 4) * 2 + g // 16
                total += jnp.where(mine == o, part[8 * g:8 * (g + 1)], 0.0)
            lt[s, :, TILE * k:TILE * (k + 1)] = total
        mark = arrival()
        for k in range(1, 4):
            go(lt.at[s], lx.at[s, k - 1], x_peer(k), mark, LOWS)
        return mark

    def low_x(s, mark):
        arrived(mark, lx.at[s])
        low_own[s] = (lt[s] + lx[s, 0]) + (lx[s, 1] + lx[s, 2])
        mark = arrival()
        for k in range(1, 4):
            go(low_own.at[s], ly.at[s, k - 1], y_peer(k), mark, LOWS)
        return mark

    def low_y(s, mark):
        arrived(mark, ly.at[s])
        total = (low_own[s] + ly[s, 0]) + (ly[s, 1] + ly[s, 2])
        low_all[s, z] = (total * weight[:, s * SR:(s + 1) * SR]).astype(BF16)
        mark = arrival()
        for k in (4, 3, 5, 2, 6, 1, 7):
            go(low_all.at[s, z], low_all.at[s, z], z_peer(k), mark, LOWS)
        return mark

    def low_z(s, mark):
        arrived(mark, low_all.at[s, pl.ds(0, 7)])
        low_t = low_all[s].astype(F32).reshape(64, SR)
        for k in range(SR // 128):
            tile = low_t[:, 128 * k:128 * (k + 1)]
            low_n[s * SR + 128 * k:s * SR + 128 * (k + 1), :] = jnp.transpose(
                jnp.concatenate([tile, tile], axis=0)
            )

    place = (x, y)
    ring_peer = (x_peer, y_peer)

    def cut(n):
        return slice(n * TILE, (n + 1) * TILE)

    lo, hi = pl.ds(0, QUART), pl.ds(QUART, QUART)

    def dots(s, h, q, first, count, emit):
        if h == 0:
            lhs = wide([tok[s, kc, pl.ds(4 * q, 4)].reshape(CR, KC) for kc in range(2)])
        else:
            lhs = wide([
                jnp.concatenate([tok[s, kc, 4 * j + q] for j in range(4)], axis=0)
                for kc in range(2)
            ])
        for n in range(first, first + count):
            cols = slice(h * HALF + n * TILE, h * HALF + (n + 1) * TILE)
            emit(n, jnp.dot(lhs, wf[:, cols], preferred_element_type=F32))

    def far(s, h):
        def put(n, v):
            s2[s, h, :, cut(n)] = v.astype(BF16)
        dots(s, h, (place[h] + 2) % 4, 0, 4, put)
        mark = arrival()
        go(s2.at[s, h, :, lo], r2.at[s, h, 0], ring_peer[h](1), mark, SUMS)
        go(s2.at[s, h, :, hi], r2.at[s, h, 1], ring_peer[h](3), mark, SUMS)
        return mark

    def near(s, h):
        def put_r(n, v):
            s1[s, h, 0, :, cut(n)] = v.astype(BF16)
        def put_l(n, v):
            s1[s, h, 1, :, cut(n)] = v.astype(BF16)
        mark = arrival()
        dots(s, h, (place[h] + 1) % 4, 2, 2, put_r)
        go(s1.at[s, h, 0, :, hi], r1.at[s, h, 0, :, hi], ring_peer[h](1), mark, SUMS)
        dots(s, h, (place[h] + 3) % 4, 0, 2, put_l)
        go(s1.at[s, h, 1, :, lo], r1.at[s, h, 1, :, lo], ring_peer[h](3), mark, SUMS)
        return mark

    def keep(s, h):
        def put(n, v):
            acc[s, h, :, cut(n)] = v
        dots(s, h, place[h], 0, 4, put)

    def relay(s, h, ready, mark):
        arrived(ready, r2.at[s, h])
        def add_r(n, v):
            s1[s, h, 0, :, cut(n)] = (v + r2[s, h, 0, :, cut(n)].astype(F32)).astype(BF16)
        def add_l(n, v):
            s1[s, h, 1, :, cut(n)] = (v + r2[s, h, 1, :, cut(n - 2)].astype(F32)).astype(BF16)
        dots(s, h, (place[h] + 1) % 4, 0, 2, add_r)
        go(s1.at[s, h, 0, :, lo], r1.at[s, h, 0, :, lo], ring_peer[h](1), mark, SUMS)
        dots(s, h, (place[h] + 3) % 4, 2, 2, add_l)
        go(s1.at[s, h, 1, :, hi], r1.at[s, h, 1, :, hi], ring_peer[h](3), mark, SUMS)

    lane = lax.broadcasted_iota(jnp.int32, (CR, 128), 1)

    def masked(s, h):
        if h == 0:
            at = pl.ds(pl.multiple_of(s * SR + x * CR, CR), CR)
            ow, lw = own_n[at, :], low_n[at, :]
        else:
            ats = [pl.ds(pl.multiple_of(s * SR + (4 * j + y) * RS, RS), RS) for j in range(4)]
            ow = jnp.concatenate([own_n[at, :] for at in ats], axis=0)
            lw = jnp.concatenate([low_n[at, :] for at in ats], axis=0)
        pieces = []
        for cc in range(2):
            for m in range(2):
                if h == 0:
                    o0, step = ((2 * m) * 4 + y) * 2 + cc, 8
                else:
                    o0, step = (x * 4 + 2 * m) * 2 + cc, 2
                want = jnp.where(lane < 64, o0, o0 + step).astype(F32)
                pieces.append(jnp.where(ow == want, lw, 0.0).astype(BF16))
        return jnp.concatenate(pieces, axis=1)

    place2 = (y, x)
    peer2 = (y_peer, x_peer)

    def block(h, q):
        return pl.ds(pl.multiple_of(q * RS, RS), RS)

    def collect(s, h, mark):
        arrived(mark, r1.at[s, h])
        lhs = masked(s, h)
        up = (bx, by)[h]
        for n in range(4):
            delta = jnp.dot(
                lhs, up[:, :, :, cut(n)].reshape(512, TILE), preferred_element_type=F32
            )
            acc[s, h, :, cut(n)] = (acc[s, h, :, cut(n)] + delta) + (
                r1[s, h, 0, :, cut(n)].astype(F32) + r1[s, h, 1, :, cut(n)].astype(F32)
            )
        mark = arrival()
        for k in (2, 1, 3):
            t1[s, h, k - 1] = acc[s, h, block(h, (place2[h] + k) % 4), :].astype(BF16)
            go(t1.at[s, h, k - 1], q1.at[s, h, k - 1], peer2[h](k), mark, SUMS)
        return mark

    def finish(s, h, mark):
        arrived(mark, q1.at[s, h])
        out_ref[s * RS:(s + 1) * RS, h * HALF:(h + 1) * HALF] = (
            (acc[s, h, block(h, place2[h]), :] + q1[s, h, 0].astype(F32))
            + (q1[s, h, 1].astype(F32) + q1[s, h, 2].astype(F32))
        ).astype(BF16)

    lows, fars, mids, ends = {}, {}, {}, {}
    for cp in tok_local:
        cp.wait()
    ring(0, 0, 0)
    for s in range(NS):
        exchange(s)
    for k in range(1, 4):
        go(a_hbm.at[z, :, a_wide((x + k) % 4)], a1.at[x], x_peer(k), a_x, START)
    go(w_hbm, wf.at[my_cols, :], partner, w_pre, START)
    ring(1, 0, 0)
    lane8 = lax.broadcasted_iota(jnp.int32, (8, 128), 1)
    per = 128 // RS
    groups = []
    for s in range(NS):
        for g in range(16 // per):
            piece = jnp.zeros((8, 128), jnp.int32)
            for j in range(per):
                d = per * g + j
                raw = jnp.broadcast_to(rows_ref[:, 128 * d:128 * (d + 1)], (8, 128))
                shift = (RS * j - RS * s + 256 - 64 * c) % 128
                piece = jnp.where(lane8 // RS == j, pltpu.roll(raw, shift, 1), piece)
            groups.append(piece[0:1])

    combo = lax.broadcasted_iota(jnp.int32, (4, 512), 1)
    hit = (ids_ref[...] - (combo // 16) * 4) == (z // 2)
    table = 0.25 * jnp.sum(jnp.where(hit, coef_ref[...], 0).astype(F32), axis=0, keepdims=True)
    column = jnp.concatenate(
        [
            jnp.transpose(jnp.broadcast_to(table[:, 128 * k:128 * (k + 1)], (128, 128)))
            for k in range(4)
        ],
        axis=0,
    )
    number = lax.broadcasted_iota(jnp.int32, (512, 128), 0)
    weight = jnp.concatenate(
        [
            jnp.sum(jnp.where(number == g, column, 0.0), axis=0, keepdims=True)
            for g in groups
        ],
        axis=1,
    )
    rows = jnp.concatenate(groups, axis=1)
    owner = rows // 16
    arrived(tok_pre[0], tok.at[0, 0, pl.ds(0, 2)])
    ring(0, 0, 1)
    owner_f = owner.astype(F32)
    for k in range(8):
        tile = jnp.broadcast_to(owner_f[:, 128 * k:128 * (k + 1)], (128, 128))
        own_n[128 * k:128 * (k + 1), :] = jnp.transpose(tile)

    arrived(tok_pre[1], tok.at[1, 0, pl.ds(0, 2)])
    ring(1, 0, 1)
    ring(0, 1, 0)
    ring(1, 1, 0)
    ring(0, 1, 1)
    ring(1, 1, 1)
    a_local.wait()
    arrived(a_x, a1.at[pl.ds(0, 3)])
    a_own = local(a1.at[:, :, a_narrow(y)], a2.at[c, y])
    for k in range(1, 4):
        go(a1.at[:, :, a_narrow((y + k) % 4)], a2.at[c, y], y_peer(k), a_y, START)
    for k in range(1, 4):
        go(b_hbm.at[:, b_cols[0]], bx.at[c, x], x_peer(k), b_x, UP)
        go(b_hbm.at[:, b_cols[1]], by.at[c, y], y_peer(k), b_y, UP)
    ring(0, 2, 0)
    ring(2, 0, 0)
    ring(1, 2, 0)
    ring(3, 0, 0)
    ring(0, 2, 1)
    arrived(tok_pre[2], tok.at[2, 0, pl.ds(0, 2)])
    ring(2, 0, 1)
    ring(1, 2, 1)
    arrived(tok_pre[3], tok.at[3, 0, pl.ds(0, 2)])
    ring(3, 0, 1)
    ring(0, 3, 0)
    ring(2, 1, 0)
    ring(1, 3, 0)
    ring(3, 1, 0)
    a_own.wait()
    arrived(a_y, a2.at[0, pl.ds(0, 3)])
    go(a2.at[c], a2.at[c], partner, a_c, START)
    ring(0, 3, 1)
    ring(2, 1, 1)
    ring(1, 3, 1)
    ring(3, 1, 1)
    ring(2, 2, 0)
    ring(3, 2, 0)
    arrived(a_c, a2.at[0])
    ring_end(0)
    lows[0] = low_part(0)
    w_local.wait()
    arrived(w_pre, wf.at[pl.ds(0, KC)])
    fars[0, 0] = far(0, 0)
    fars[0, 1] = far(0, 1)
    mids[0, 0] = near(0, 0)
    ring(2, 2, 1)
    mids[0, 1] = near(0, 1)
    for cp in b_local:
        cp.wait()
    arrived(b_x, bx.at[0, pl.ds(0, 3)])
    arrived(b_y, by.at[0, pl.ds(0, 3)])
    for ref in (bx, by):
        go(ref.at[c], ref.at[c], partner, b_c, UP)
    keep(0, 0)
    ring_end(1)
    lows[1] = low_part(1)
    fars[1, 1] = far(1, 1)
    fars[1, 0] = far(1, 0)
    mids[1, 1] = near(1, 1)
    ring(3, 2, 1)
    mids[1, 0] = near(1, 0)
    keep(0, 1)
    keep(1, 1)
    keep(1, 0)
    ring(2, 3, 0)
    ring(3, 3, 0)
    lows[0] = low_x(0, lows[0])
    ring(2, 3, 1)
    relay(0, 0, fars[0, 0], mids[0, 0])
    relay(0, 1, fars[0, 1], mids[0, 1])
    ring(3, 3, 1)
    lows[1] = low_x(1, lows[1])
    ring_end(2)
    lows[2] = low_part(2)
    relay(1, 0, fars[1, 0], mids[1, 0])
    relay(1, 1, fars[1, 1], mids[1, 1])
    fars[2, 1] = far(2, 1)
    fars[2, 0] = far(2, 0)
    mids[2, 1] = near(2, 1)
    ring_end(3)
    lows[3] = low_part(3)
    mids[2, 0] = near(2, 0)
    fars[3, 1] = far(3, 1)
    fars[3, 0] = far(3, 0)
    mids[3, 1] = near(3, 1)
    mids[3, 0] = near(3, 0)
    keep(2, 1)
    keep(2, 0)
    keep(3, 0)
    lows[0] = low_y(0, lows[0])
    keep(3, 1)
    lows[2] = low_x(2, lows[2])
    lows[1] = low_y(1, lows[1])
    relay(2, 0, fars[2, 0], mids[2, 0])
    relay(2, 1, fars[2, 1], mids[2, 1])
    lows[3] = low_x(3, lows[3])
    low_z(0, lows[0])
    arrived(b_c, bx)
    ends[0, 1] = collect(0, 1, mids[0, 1])
    relay(3, 1, fars[3, 1], mids[3, 1])
    relay(3, 0, fars[3, 0], mids[3, 0])
    ends[0, 0] = collect(0, 0, mids[0, 0])
    low_z(1, lows[1])
    ends[1, 0] = collect(1, 0, mids[1, 0])
    ends[1, 1] = collect(1, 1, mids[1, 1])
    lows[2] = low_y(2, lows[2])
    lows[3] = low_y(3, lows[3])
    finish(0, 1, ends[0, 1])
    finish(0, 0, ends[0, 0])
    finish(1, 1, ends[1, 1])
    finish(1, 0, ends[1, 0])
    low_z(2, lows[2])
    ends[2, 1] = collect(2, 1, mids[2, 1])
    ends[2, 0] = collect(2, 0, mids[2, 0])
    low_z(3, lows[3])
    ends[3, 1] = collect(3, 1, mids[3, 1])
    ends[3, 0] = collect(3, 0, mids[3, 0])
    finish(2, 1, ends[2, 1])
    finish(2, 0, ends[2, 0])
    finish(3, 1, ends[3, 1])
    finish(3, 0, ends[3, 0])
    for group in (START, UP, RING, SUMS):
        gone(group, wf)
    gone(LOWS, own_n)


def body(tokens, query_weight, down, up, request_combination, task_ids, coefficient):
    hbm = pl.BlockSpec(memory_space=pl.ANY)
    vmem = pl.BlockSpec(memory_space=pltpu.VMEM)
    n_sem = 79
    return pl.pallas_call(
        kernel,
        out_shape=jax.ShapeDtypeStruct((64, 2048), BF16),
        in_specs=[hbm, hbm, hbm, hbm, vmem, vmem, vmem],
        out_specs=vmem,
        scratch_shapes=[
            pltpu.VMEM((NS, 2, 16, RS, KC), BF16),
            pltpu.VMEM((1024, 2048), BF16),
            pltpu.VMEM((4, 8, 4096), BF16),
            pltpu.VMEM((2, 4, 4, 8, 1024), BF16),
            pltpu.VMEM((2, 4, 64, HALF), BF16),
            pltpu.VMEM((2, 4, 64, HALF), BF16),
            pltpu.VMEM((1024, 128), F32),
            pltpu.VMEM((1024, 128), F32),
            pltpu.VMEM((NS, 8, SR), F32),
            pltpu.VMEM((NS, 3, 8, SR), F32),
            pltpu.VMEM((NS, 3, 8, SR), F32),
            pltpu.VMEM((NS, 8, SR), F32),
            pltpu.VMEM((NS, 8, 8, SR), BF16),
            pltpu.VMEM((NS, 2, CR, HALF), BF16),
            pltpu.VMEM((NS, 2, 2, CR, QUART), BF16),
            pltpu.VMEM((NS, 2, 2, CR, HALF), BF16),
            pltpu.VMEM((NS, 2, 2, CR, HALF), BF16),
            pltpu.VMEM((NS, 2, CR, HALF), F32),
            pltpu.VMEM((NS, 2, 3, RS, HALF), BF16),
            pltpu.VMEM((NS, 2, 3, RS, HALF), BF16),
            pltpu.SemaphoreType.DMA((5,)),
            pltpu.SemaphoreType.DMA((n_sem,)),
            pltpu.SemaphoreType.DMA((NS + 5,)),
        ],
        compiler_params=pltpu.CompilerParams(
            collective_id=0, has_side_effects=True, vmem_limit_bytes=67043328
        ),
    )(
        tokens.reshape(2, 2, NS, RS, KC),
        query_weight,
        down.reshape(8, 8, 16384),
        up.reshape(64, 16384),
        request_combination.reshape(1, 2048),
        task_ids.T,
        coefficient.T,
    )


def solution(mesh):
    placed = (
        P("tensor", "adapter"),
        P("adapter", "tensor"),
        P("adapter", None, None),
        P("adapter", None, None),
        P(),
        P(),
        P(),
    )
    return jax.shard_map(
        body, mesh=mesh, in_specs=placed, out_specs=P("adapter", "tensor"), check_vma=False
    )
```

time: 70.3 us -> 66.7 us (0.949)
  Pallas kernels: 68.5 us -> 64.2 us
    pallas_call x1, Pallas kernels: 68.5 us -> 64.2 us  [body(): pl.pallas_call(kernel, out_shape=jax.ShapeDtypeStruct((64, 2048), BF16),...]
where the time goes in v5:
time: 66.7 us; the launch traced here: 65.9 us
  Pallas kernels  64.2 us (96%)
  local copies, waits for them, and re-layouts  1.67 us (3%)
    pallas_call x1, Pallas kernels, body(): pl.pallas_call(kernel, out_shape=jax.ShapeDtypeStruct((64, 2048), BF16),...  64.2 us
    unnamed x1, local copies, waits for them, and re-layouts  1.67 us

profile of v5, /device:TPU:2, one launch (start us, length us, event | category | flops | bytes accessed | tf_op | source)
XLA Modules:
  0.0 65.9 jit_solution(6884846060914635272)
XLA Ops:
  0.0 64.2 %shard_map.73 = bf16[64,2048]{1,0:T(8,128)(2,1)} custom-call(bf16[2,2,4,16,512]{4,3,2,1,0:T(8,128)(2,1)} %bitcast.8, bf16[512,2048]{1,0:T(8,128)(2,1)} %w_hbm.1, bf16[8,8,16384]{2,1,0:T(8,128)(2,1)} %bitcast.6, bf16[64,16384]{1,0:T(8,128)(2,1)} %bitcast.7, s32[1,2048]{1,0:T(1,128)} %bitcast.9, s32[4,512]{1,0:T(4,128)} %bitcast.10, s32[4,512]{1,0:T(4,128)} %bitcast.11), custom_call_target="tpu_custom_call" | custom-call | tf_op jit(solution)/shard_map/pallas_call | solution.py:470
  64.2 1.7 %copy.9 = bf16[64,2048]{1,0:T(8,128)(2,1)} copy(bf16[64,2048]{1,0:T(8,128)(2,1)} %shard_map.73) | data formatting | bytes 524288

commit v6 on v5

--- a/solution.py
+++ b/solution.py
@@ -7,10 +7,12 @@
 from jax.experimental.pallas import tpu as pltpu
 from jax.sharding import PartitionSpec as P
 
-NS = 4
+NS = 2
 RS = 64 // NS
 SR = 16 * RS
 CR = 4 * RS
+NR = 8 * RS
+PB = 64 // RS
 KC = 512
 HALF = 1024
 QUART = 512
@@ -47,6 +49,7 @@
         return dev(x, y, c, (z + k) % 8)
 
     partner = dev(x, y, other, z)
+    task = z % 4
     counter = [0, 0]
     sent = [0] * 5
     START, UP, RING, SUMS, LOWS = range(5)
@@ -89,7 +92,7 @@
     ]
     a_wide = lambda xx: pl.ds(pl.multiple_of(xx * 4096, 4096), 4096)
     a_narrow = lambda yy: pl.ds(pl.multiple_of(yy * 1024, 1024), 1024)
-    a_local = local(a_hbm.at[z, :, a_wide(x)], a1.at[x])
+    a_local = local(a_hbm.at[task, :, a_wide(x)], a1.at[x])
     b_cols = [pl.ds(pl.multiple_of(z * 2048 + h * HALF, HALF), HALF) for h in range(2)]
     b_local = [
         local(b_hbm.at[:, b_cols[0]], bx.at[c, x]),
@@ -131,23 +134,29 @@
         for u in range(2):
             arrived(moving.pop((s, 3, u)), tok.at[s, 0, pl.ds(0, 2)])
 
+    near_block = [(z + 7 + j) % 8 for j in range(4)]
+
     def wide(halves):
         return jnp.concatenate(halves, axis=1)
 
     def low_part(s):
-        af = a2[...].reshape(256, 1024)
-        for k in range(SR // TILE):
-            nd = TILE // RS
+        af = a2[...].reshape(512, 1024)
+        for v in range(NR // 128):
+            blocks = near_block[PB * v:PB * (v + 1)]
+            rhs = wide([
+                jnp.concatenate(
+                    [tok[s, kc, pl.ds(2 * b, 2)].reshape(2 * RS, KC) for b in blocks], axis=0
+                )
+                for kc in range(2)
+            ])
             part = lax.dot_general(
-                af, wide([tok[s, kc, nd * k:nd * (k + 1)].reshape(TILE, KC) for kc in range(2)]),
-                (((1,), (1,)), ((), ())), preferred_element_type=F32,
+                af, rhs, (((1,), (1,)), ((), ())), preferred_element_type=F32
             )
-            mine = owner[:, s * SR + TILE * k:s * SR + TILE * (k + 1)]
-            total = jnp.zeros((8, TILE), F32)
+            total = jnp.zeros((16, 128), F32)
             for g in range(32):
                 o = ((g % 4) * 4 + (g // 4) % 4) * 2 + g // 16
-                total += jnp.where(mine == o, part[8 * g:8 * (g + 1)], 0.0)
-            lt[s, :, TILE * k:TILE * (k + 1)] = total
+                total += jnp.where(near_owner[s][v] == o, part[16 * g:16 * (g + 1)], 0.0)
+            lt[s, :, 128 * v:128 * (v + 1)] = total
         mark = arrival()
         for k in range(1, 4):
             go(lt.at[s], lx.at[s, k - 1], x_peer(k), mark, LOWS)
@@ -164,7 +173,7 @@
     def low_y(s, mark):
         arrived(mark, ly.at[s])
         total = (low_own[s] + ly[s, 0]) + (ly[s, 1] + ly[s, 2])
-        low_all[s, z] = (total * weight[:, s * SR:(s + 1) * SR]).astype(BF16)
+        low_all[s, z] = (total * weight[s]).astype(BF16)
         mark = arrival()
         for k in (4, 3, 5, 2, 6, 1, 7):
             go(low_all.at[s, z], low_all.at[s, z], z_peer(k), mark, LOWS)
@@ -172,12 +181,24 @@
 
     def low_z(s, mark):
         arrived(mark, low_all.at[s, pl.ds(0, 7)])
-        low_t = low_all[s].astype(F32).reshape(64, SR)
-        for k in range(SR // 128):
-            tile = low_t[:, 128 * k:128 * (k + 1)]
-            low_n[s * SR + 128 * k:s * SR + 128 * (k + 1), :] = jnp.transpose(
-                jnp.concatenate([tile, tile], axis=0)
-            )
+        group = lax.broadcasted_iota(jnp.int32, (16, 128), 1) // (2 * RS)
+        for m in range(8 // PB):
+            parts = []
+            for t in range(4):
+                piece = jnp.zeros((16, 128), F32)
+                for bl in range(PB):
+                    b = PB * m + bl
+                    zz, j = [
+                        (v % 8, b - v + 1) for v in range(b - 2, b + 2) if v % 4 == t
+                    ][0]
+                    lanes = slice(128 * (j // PB), 128 * (j // PB) + 128)
+                    moved = pltpu.roll(
+                        low_all[s, zz, :, lanes].astype(F32), (2 * RS * (bl - j % PB)) % 128, 1
+                    )
+                    piece = jnp.where(group == bl, moved, piece)
+                parts.append(piece)
+            at = s * SR + 128 * m
+            low_n[at:at + 128, :] = jnp.transpose(jnp.concatenate(parts + parts, axis=0))
 
     place = (x, y)
     ring_peer = (x_peer, y_peer)
@@ -294,24 +315,21 @@
     for s in range(NS):
         exchange(s)
     for k in range(1, 4):
-        go(a_hbm.at[z, :, a_wide((x + k) % 4)], a1.at[x], x_peer(k), a_x, START)
+        go(a_hbm.at[task, :, a_wide((x + k) % 4)], a1.at[x], x_peer(k), a_x, START)
     go(w_hbm, wf.at[my_cols, :], partner, w_pre, START)
-    ring(1, 0, 0)
     lane8 = lax.broadcasted_iota(jnp.int32, (8, 128), 1)
-    per = 128 // RS
-    groups = []
-    for s in range(NS):
-        for g in range(16 // per):
-            piece = jnp.zeros((8, 128), jnp.int32)
-            for j in range(per):
-                d = per * g + j
-                raw = jnp.broadcast_to(rows_ref[:, 128 * d:128 * (d + 1)], (8, 128))
-                shift = (RS * j - RS * s + 256 - 64 * c) % 128
-                piece = jnp.where(lane8 // RS == j, pltpu.roll(raw, shift, 1), piece)
-            groups.append(piece[0:1])
+
+    def numbers(s, ds):
+        piece = jnp.zeros((8, 128), jnp.int32)
+        for j, d in enumerate(ds):
+            raw = rows_ref[:, pl.ds(pl.multiple_of(128 * d, 128), 128)]
+            raw = jnp.broadcast_to(raw, (8, 128))
+            shift = (RS * j - RS * s + 256 - 64 * c) % 128
+            piece = jnp.where(lane8 // RS == j, pltpu.roll(raw, shift, 1), piece)
+        return piece[0:1]
 
     combo = lax.broadcasted_iota(jnp.int32, (4, 512), 1)
-    hit = (ids_ref[...] - (combo // 16) * 4) == (z // 2)
+    hit = (ids_ref[...] - (combo // 16) * 4) == task
     table = 0.25 * jnp.sum(jnp.where(hit, coef_ref[...], 0).astype(F32), axis=0, keepdims=True)
     column = jnp.concatenate(
         [
@@ -321,28 +339,34 @@
         axis=0,
     )
     number = lax.broadcasted_iota(jnp.int32, (512, 128), 0)
-    weight = jnp.concatenate(
-        [
-            jnp.sum(jnp.where(number == g, column, 0.0), axis=0, keepdims=True)
-            for g in groups
-        ],
-        axis=1,
-    )
-    rows = jnp.concatenate(groups, axis=1)
-    owner = rows // 16
+    per = 128 // RS
+    near_d = [2 * b + jj for b in near_block for jj in range(2)]
+    near_rows = [
+        [numbers(s, near_d[per * v:per * (v + 1)]) for v in range(NR // 128)] for s in range(NS)
+    ]
+    near_owner = [[rows // 16 for rows in stage] for stage in near_rows]
+    weight = [
+        jnp.concatenate(
+            [
+                jnp.sum(jnp.where(number == rows, column, 0.0), axis=0, keepdims=True)
+                for rows in stage
+            ],
+            axis=1,
+        )
+        for stage in near_rows
+    ]
     arrived(tok_pre[0], tok.at[0, 0, pl.ds(0, 2)])
     ring(0, 0, 1)
-    owner_f = owner.astype(F32)
-    for k in range(8):
-        tile = jnp.broadcast_to(owner_f[:, 128 * k:128 * (k + 1)], (128, 128))
-        own_n[128 * k:128 * (k + 1), :] = jnp.transpose(tile)
-
-    arrived(tok_pre[1], tok.at[1, 0, pl.ds(0, 2)])
-    ring(1, 0, 1)
+    for s in range(NS):
+        for m in range(SR // 128):
+            owner = numbers(s, range(per * m, per * (m + 1))) // 16
+            tile = jnp.broadcast_to(owner.astype(F32), (128, 128))
+            at = s * SR + 128 * m
+            own_n[at:at + 128, :] = jnp.transpose(tile)
     ring(0, 1, 0)
-    ring(1, 1, 0)
     ring(0, 1, 1)
-    ring(1, 1, 1)
+    ring(0, 2, 0)
+    ring(1, 0, 0)
     a_local.wait()
     arrived(a_x, a1.at[pl.ds(0, 3)])
     a_own = local(a1.at[:, :, a_narrow(y)], a2.at[c, y])
@@ -351,113 +375,64 @@
     for k in range(1, 4):
         go(b_hbm.at[:, b_cols[0]], bx.at[c, x], x_peer(k), b_x, UP)
         go(b_hbm.at[:, b_cols[1]], by.at[c, y], y_peer(k), b_y, UP)
-    ring(0, 2, 0)
-    ring(2, 0, 0)
-    ring(1, 2, 0)
-    ring(3, 0, 0)
     ring(0, 2, 1)
-    arrived(tok_pre[2], tok.at[2, 0, pl.ds(0, 2)])
-    ring(2, 0, 1)
-    ring(1, 2, 1)
-    arrived(tok_pre[3], tok.at[3, 0, pl.ds(0, 2)])
-    ring(3, 0, 1)
+    arrived(tok_pre[1], tok.at[1, 0, pl.ds(0, 2)])
+    ring(1, 0, 1)
     ring(0, 3, 0)
-    ring(2, 1, 0)
-    ring(1, 3, 0)
-    ring(3, 1, 0)
+    ring(1, 1, 0)
+    ring(0, 3, 1)
+    ring(1, 1, 1)
     a_own.wait()
     arrived(a_y, a2.at[0, pl.ds(0, 3)])
     go(a2.at[c], a2.at[c], partner, a_c, START)
-    ring(0, 3, 1)
-    ring(2, 1, 1)
-    ring(1, 3, 1)
-    ring(3, 1, 1)
-    ring(2, 2, 0)
-    ring(3, 2, 0)
-    arrived(a_c, a2.at[0])
-    ring_end(0)
-    lows[0] = low_part(0)
+    ring(1, 2, 0)
     w_local.wait()
     arrived(w_pre, wf.at[pl.ds(0, KC)])
+    ring_end(0)
     fars[0, 0] = far(0, 0)
     fars[0, 1] = far(0, 1)
     mids[0, 0] = near(0, 0)
-    ring(2, 2, 1)
     mids[0, 1] = near(0, 1)
+    keep(0, 1)
+    keep(0, 0)
+    arrived(a_c, a2.at[0])
+    lows[0] = low_part(0)
+    ring(1, 2, 1)
+    lows[1] = low_part(1)
+    ring(1, 3, 0)
     for cp in b_local:
         cp.wait()
     arrived(b_x, bx.at[0, pl.ds(0, 3)])
     arrived(b_y, by.at[0, pl.ds(0, 3)])
     for ref in (bx, by):
         go(ref.at[c], ref.at[c], partner, b_c, UP)
-    keep(0, 0)
+    relay(0, 0, fars[0, 0], mids[0, 0])
+    ring(1, 3, 1)
+    relay(0, 1, fars[0, 1], mids[0, 1])
     ring_end(1)
-    lows[1] = low_part(1)
     fars[1, 1] = far(1, 1)
     fars[1, 0] = far(1, 0)
+    lows[0] = low_x(0, lows[0])
     mids[1, 1] = near(1, 1)
-    ring(3, 2, 1)
+    lows[1] = low_x(1, lows[1])
     mids[1, 0] = near(1, 0)
-    keep(0, 1)
+    keep(1, 0)
     keep(1, 1)
-    keep(1, 0)
-    ring(2, 3, 0)
-    ring(3, 3, 0)
-    lows[0] = low_x(0, lows[0])
-    ring(2, 3, 1)
-    relay(0, 0, fars[0, 0], mids[0, 0])
-    relay(0, 1, fars[0, 1], mids[0, 1])
-    ring(3, 3, 1)
-    lows[1] = low_x(1, lows[1])
-    ring_end(2)
-    lows[2] = low_part(2)
+    relay(1, 1, fars[1, 1], mids[1, 1])
     relay(1, 0, fars[1, 0], mids[1, 0])
-    relay(1, 1, fars[1, 1], mids[1, 1])
-    fars[2, 1] = far(2, 1)
-    fars[2, 0] = far(2, 0)
-    mids[2, 1] = near(2, 1)
-    ring_end(3)
-    lows[3] = low_part(3)
-    mids[2, 0] = near(2, 0)
-    fars[3, 1] = far(3, 1)
-    fars[3, 0] = far(3, 0)
-    mids[3, 1] = near(3, 1)
-    mids[3, 0] = near(3, 0)
-    keep(2, 1)
-    keep(2, 0)
-    keep(3, 0)
     lows[0] = low_y(0, lows[0])
-    keep(3, 1)
-    lows[2] = low_x(2, lows[2])
     lows[1] = low_y(1, lows[1])
-    relay(2, 0, fars[2, 0], mids[2, 0])
-    relay(2, 1, fars[2, 1], mids[2, 1])
-    lows[3] = low_x(3, lows[3])
     low_z(0, lows[0])
     arrived(b_c, bx)
+    ends[0, 0] = collect(0, 0, mids[0, 0])
     ends[0, 1] = collect(0, 1, mids[0, 1])
-    relay(3, 1, fars[3, 1], mids[3, 1])
-    relay(3, 0, fars[3, 0], mids[3, 0])
-    ends[0, 0] = collect(0, 0, mids[0, 0])
     low_z(1, lows[1])
+    ends[1, 1] = collect(1, 1, mids[1, 1])
     ends[1, 0] = collect(1, 0, mids[1, 0])
-    ends[1, 1] = collect(1, 1, mids[1, 1])
-    lows[2] = low_y(2, lows[2])
-    lows[3] = low_y(3, lows[3])
+    finish(0, 0, ends[0, 0])
     finish(0, 1, ends[0, 1])
-    finish(0, 0, ends[0, 0])
     finish(1, 1, ends[1, 1])
     finish(1, 0, ends[1, 0])
-    low_z(2, lows[2])
-    ends[2, 1] = collect(2, 1, mids[2, 1])
-    ends[2, 0] = collect(2, 0, mids[2, 0])
-    low_z(3, lows[3])
-    ends[3, 1] = collect(3, 1, mids[3, 1])
-    ends[3, 0] = collect(3, 0, mids[3, 0])
-    finish(2, 1, ends[2, 1])
-    finish(2, 0, ends[2, 0])
-    finish(3, 1, ends[3, 1])
-    finish(3, 0, ends[3, 0])
     for group in (START, UP, RING, SUMS):
         gone(group, wf)
     gone(LOWS, own_n)
@@ -466,7 +441,7 @@
 def body(tokens, query_weight, down, up, request_combination, task_ids, coefficient):
     hbm = pl.BlockSpec(memory_space=pl.ANY)
     vmem = pl.BlockSpec(memory_space=pltpu.VMEM)
-    n_sem = 79
+    n_sem = 43
     return pl.pallas_call(
         kernel,
         out_shape=jax.ShapeDtypeStruct((64, 2048), BF16),
@@ -475,17 +450,17 @@
         scratch_shapes=[
             pltpu.VMEM((NS, 2, 16, RS, KC), BF16),
             pltpu.VMEM((1024, 2048), BF16),
-            pltpu.VMEM((4, 8, 4096), BF16),
-            pltpu.VMEM((2, 4, 4, 8, 1024), BF16),
+            pltpu.VMEM((4, 16, 4096), BF16),
+            pltpu.VMEM((2, 4, 4, 16, 1024), BF16),
             pltpu.VMEM((2, 4, 64, HALF), BF16),
             pltpu.VMEM((2, 4, 64, HALF), BF16),
             pltpu.VMEM((1024, 128), F32),
             pltpu.VMEM((1024, 128), F32),
-            pltpu.VMEM((NS, 8, SR), F32),
-            pltpu.VMEM((NS, 3, 8, SR), F32),
-            pltpu.VMEM((NS, 3, 8, SR), F32),
-            pltpu.VMEM((NS, 8, SR), F32),
-            pltpu.VMEM((NS, 8, 8, SR), BF16),
+            pltpu.VMEM((NS, 16, NR), F32),
+            pltpu.VMEM((NS, 3, 16, NR), F32),
+            pltpu.VMEM((NS, 3, 16, NR), F32),
+            pltpu.VMEM((NS, 16, NR), F32),
+            pltpu.VMEM((NS, 8, 16, NR), BF16),
             pltpu.VMEM((NS, 2, CR, HALF), BF16),
             pltpu.VMEM((NS, 2, 2, CR, QUART), BF16),
             pltpu.VMEM((NS, 2, 2, CR, HALF), BF16),
@@ -503,7 +478,7 @@
     )(
         tokens.reshape(2, 2, NS, RS, KC),
         query_weight,
-        down.reshape(8, 8, 16384),
+        down,
         up.reshape(64, 16384),
         request_combination.reshape(1, 2048),
         task_ids.T,

time: 66.7 us -> 61.7 us (0.925)
  Pallas kernels: 64.2 us -> 59.4 us
    pallas_call x1, Pallas kernels: 64.2 us -> 59.4 us  [body(): pl.pallas_call(kernel, out_shape=jax.ShapeDtypeStruct((64, 2048), BF16),...]
where the time goes in v6:
time: 61.7 us; the launch traced here: 61.1 us
  Pallas kernels  59.4 us (96%)
  local copies, waits for them, and re-layouts  1.67 us (3%)
    pallas_call x1, Pallas kernels, body(): pl.pallas_call(kernel, out_shape=jax.ShapeDtypeStruct((64, 2048), BF16),...  59.4 us
    unnamed x1, local copies, waits for them, and re-layouts  1.67 us

profile of v6, /device:TPU:2, one launch (start us, length us, event | category | flops | bytes accessed | tf_op | source)
XLA Modules:
  0.0 61.1 jit_solution(1064417865393895394)
XLA Ops:
  0.0 59.4 %shard_map.73 = bf16[64,2048]{1,0:T(8,128)(2,1)} custom-call(bf16[2,2,2,32,512]{4,3,2,1,0:T(8,128)(2,1)} %bitcast.6, bf16[512,2048]{1,0:T(8,128)(2,1)} %w_hbm.1, bf16[4,16,16384]{2,1,0:T(8,128)(2,1)} %a_hbm.1, bf16[64,16384]{1,0:T(8,128)(2,1)} %bitcast.5, s32[1,2048]{1,0:T(1,128)} %bitcast.7, s32[4,512]{1,0:T(4,128)} %bitcast.8, s32[4,512]{1,0:T(4,128)} %bitcast.9), custom_call_target="tpu_custom_call" | custom-call | tf_op jit(solution)/shard_map/pallas_call | solution.py:445
  59.5 1.7 %copy.9 = bf16[64,2048]{1,0:T(8,128)(2,1)} copy(bf16[64,2048]{1,0:T(8,128)(2,1)} %shard_map.73) | data formatting | bytes 524288

commit v7 on v6

--- a/solution.py
+++ b/solution.py
@@ -391,46 +391,46 @@
     ring_end(0)
     fars[0, 0] = far(0, 0)
     fars[0, 1] = far(0, 1)
-    mids[0, 0] = near(0, 0)
     mids[0, 1] = near(0, 1)
-    keep(0, 1)
-    keep(0, 0)
     arrived(a_c, a2.at[0])
     lows[0] = low_part(0)
+    mids[0, 0] = near(0, 0)
+    keep(0, 0)
+    keep(0, 1)
     ring(1, 2, 1)
     lows[1] = low_part(1)
-    ring(1, 3, 0)
     for cp in b_local:
         cp.wait()
     arrived(b_x, bx.at[0, pl.ds(0, 3)])
     arrived(b_y, by.at[0, pl.ds(0, 3)])
     for ref in (bx, by):
         go(ref.at[c], ref.at[c], partner, b_c, UP)
+    ring(1, 3, 0)
     relay(0, 0, fars[0, 0], mids[0, 0])
+    relay(0, 1, fars[0, 1], mids[0, 1])
     ring(1, 3, 1)
-    relay(0, 1, fars[0, 1], mids[0, 1])
+    lows[0] = low_x(0, lows[0])
+    lows[1] = low_x(1, lows[1])
     ring_end(1)
     fars[1, 1] = far(1, 1)
     fars[1, 0] = far(1, 0)
-    lows[0] = low_x(0, lows[0])
     mids[1, 1] = near(1, 1)
-    lows[1] = low_x(1, lows[1])
     mids[1, 0] = near(1, 0)
     keep(1, 0)
     keep(1, 1)
+    lows[0] = low_y(0, lows[0])
+    lows[1] = low_y(1, lows[1])
     relay(1, 1, fars[1, 1], mids[1, 1])
     relay(1, 0, fars[1, 0], mids[1, 0])
-    lows[0] = low_y(0, lows[0])
-    lows[1] = low_y(1, lows[1])
     low_z(0, lows[0])
     arrived(b_c, bx)
+    ends[0, 1] = collect(0, 1, mids[0, 1])
     ends[0, 0] = collect(0, 0, mids[0, 0])
-    ends[0, 1] = collect(0, 1, mids[0, 1])
     low_z(1, lows[1])
     ends[1, 1] = collect(1, 1, mids[1, 1])
     ends[1, 0] = collect(1, 0, mids[1, 0])
+    finish(0, 1, ends[0, 1])
     finish(0, 0, ends[0, 0])
-    finish(0, 1, ends[0, 1])
     finish(1, 1, ends[1, 1])
     finish(1, 0, ends[1, 0])
     for group in (START, UP, RING, SUMS):

time: 61.7 us -> 59.8 us (0.969); the launches traced: 61.1 us -> 58.6 us
  Pallas kernels: 59.4 us -> 56.9 us
    pallas_call x1, Pallas kernels: 59.4 us -> 56.9 us  [body(): pl.pallas_call(kernel, out_shape=jax.ShapeDtypeStruct((64, 2048), BF16),...]
where the time goes in v7:
time: 59.8 us; the launch traced here: 58.6 us
  Pallas kernels  56.9 us (95%)
  local copies, waits for them, and re-layouts  1.67 us (3%)
    pallas_call x1, Pallas kernels, body(): pl.pallas_call(kernel, out_shape=jax.ShapeDtypeStruct((64, 2048), BF16),...  56.9 us
    unnamed x1, local copies, waits for them, and re-layouts  1.67 us

profile of v7, /device:TPU:2, one launch (start us, length us, event | category | flops | bytes accessed | tf_op | source)
XLA Modules:
  0.0 58.6 jit_solution(4679451458974417414)
XLA Ops:
  0.0 56.9 %shard_map.73 = bf16[64,2048]{1,0:T(8,128)(2,1)} custom-call(bf16[2,2,2,32,512]{4,3,2,1,0:T(8,128)(2,1)} %bitcast.6, bf16[512,2048]{1,0:T(8,128)(2,1)} %w_hbm.1, bf16[4,16,16384]{2,1,0:T(8,128)(2,1)} %a_hbm.1, bf16[64,16384]{1,0:T(8,128)(2,1)} %bitcast.5, s32[1,2048]{1,0:T(1,128)} %bitcast.7, s32[4,512]{1,0:T(4,128)} %bitcast.8, s32[4,512]{1,0:T(4,128)} %bitcast.9), custom_call_target="tpu_custom_call" | custom-call | tf_op jit(solution)/shard_map/pallas_call | solution.py:445
  56.9 1.7 %copy.9 = bf16[64,2048]{1,0:T(8,128)(2,1)} copy(bf16[64,2048]{1,0:T(8,128)(2,1)} %shard_map.73) | data formatting | bytes 524288
